TPU v7x, 32 devices: a whole 2x2x4 slice. The times are simulated.
32 devices in a mesh: angle: 4 (over y, x), panel: 8 (over z, core).
Axes of the slice: x: 2, y: 2, z: 4, core: 2. Of those that a mesh axis runs over, the one named last changes fastest.
Arguments:
- measured: bfloat16 [64, 512, 1024], P(('angle', 'panel')), may hold values from 0.099609375 to 1
- predicted: bfloat16 [64, 512, 1024], P(('angle', 'panel')), may hold values from 0 to 2
- slice_filter: bfloat16 [512, 512], replicated, may hold values from -0.25 to 0.25
- column_filter: bfloat16 [1024, 1024], replicated, may hold values from -0.1875 to 0.1875
- volume: float32 [512, 16384], P('angle', 'panel'), may hold values from 0 to 1
- tiles: bfloat16 [1536, 128, 128], P('panel'), may hold values from -0.5 to 0.5
- tile_ray: int32 [1536], P('panel'), may hold values from 0 to 63
- tile_vox: int32 [1536], P('panel'), may hold values from 0 to 127
- live_tiles: int32 [8], P('panel'), may hold values from 1 to 192, as said below
Outputs:
- updated_volume: float32 [512, 16384], P('angle', 'panel')
- projected: bfloat16 [64, 512, 1024], P(('angle', 'panel'))
Inputs may be any that keep to these rules, and one draw needn't show every extreme that they name: live_tiles[p] counts the tile slots of panel p that are used, from the first slot on; at least one panel uses all 192 slots.
All inputs are finite; a program needn't handle non-finite values.
Results may differ from a plain program's by a relative error of at most 0.0065.
Values may be sent and summed in bfloat16 or wider, within the bound.
No kernel may reach another device: no remote copies, remote signals or barrier semaphores. Data moves between devices by JAX's collectives and lax.ppermute only.
A program may use at most 128 MiB of HBM per device.

v0:
```python
import functools

import jax
import jax.numpy as jnp
from jax import lax
from jax.experimental import pallas as pl
from jax.experimental.pallas import tpu as pltpu
from jax.sharding import PartitionSpec as P


step_size = 0.1
LANES = 128
UNROLL = 48
AHEAD = 4
FILTER_STEPS = 2
CUTS = (1, 1)
MIB = 1024 * 1024


VMEM_SPEC = pl.BlockSpec(memory_space=pltpu.VMEM)
ANY_SPEC = pl.BlockSpec(memory_space=pl.ANY)
HBM_SPEC = pl.BlockSpec(memory_space=pltpu.HBM)
SMEM_SPEC = pl.BlockSpec(memory_space=pltpu.SMEM)


def params(mib):
    return pltpu.CompilerParams(vmem_limit_bytes=mib * MIB)


def row_parts(rows_dev):
    cuts = CUTS
    while len(cuts) > 1 and rows_dev * min(cuts) < 16 * sum(cuts):
        cuts = (1,) * (len(cuts) - 1)
    return [rows_dev * cut // sum(cuts) for cut in cuts]


def swap_bits(panels):
    return [1 << b for b in range(panels.bit_length() - 1)]


def swap_mask(index, step, bits):
    far = bits[1:]
    return far[step] if index % 2 == 0 else far[len(far) - 1 - step]


def swap_far(value, step, bits):
    size = lax.axis_size("panel")
    return lax.ppermute(value, "panel", [(i, i ^ swap_mask(i, step, bits)) for i in range(size)])


def cost(us):
    return pl.CostEstimate(flops=int(us * 1e9), bytes_accessed=0, transcendentals=0)


def swap(value, axis, mask):
    size = lax.axis_size(axis)
    return lax.ppermute(value, axis, [(i, i ^ mask) for i in range(size)])


def filter_rows(slice_ref, start_of, across, outs, angle, rows):
    picked = jnp.concatenate(
        [slice_ref[pl.ds(pl.multiple_of(start_of(m), 16), rows), :] for m in range(len(outs))], axis=0
    )
    result = jnp.dot(picked, across, preferred_element_type=jnp.float32).astype(jnp.bfloat16)
    for m, out in enumerate(outs):
        out[angle] = result[m * rows : (m + 1) * rows]


def first_filter_kernel(rows, start_of, measured, predicted, slice_ref, column_ref, across_out, *refs):
    outs = refs[:-5]
    measured_scr, predicted_scr, slice_scr, column_scr, sems = refs[-5:]
    held, slices, _ = measured.shape
    step = slices // FILTER_STEPS
    places = [(angle, pl.ds(i * step, step)) for angle in range(held) for i in range(FILTER_STEPS)]
    pairs = [
        [
            pltpu.make_async_copy(predicted.at[place], predicted_scr.at[place], sems.at[2 * i]),
            pltpu.make_async_copy(measured.at[place], measured_scr.at[place], sems.at[2 * i + 1]),
        ]
        for i, place in enumerate(places)
    ]
    column_copy = pltpu.make_async_copy(column_ref, column_scr, sems.at[2 * len(places)])
    slice_copy = pltpu.make_async_copy(slice_ref, slice_scr, sems.at[2 * len(places) + 1])
    for copy in pairs[0] + [column_copy]:
        copy.start()
    for i, (angle, part) in enumerate(places):
        for copy in pairs[i]:
            copy.wait()
        if i == 0:
            for copy in sum(pairs[1:], []) + [slice_copy]:
                copy.start()
        bright = jnp.exp(-predicted_scr[angle, part].astype(jnp.float32))
        misfit = ((measured_scr[angle, part].astype(jnp.float32) - bright) * bright).astype(jnp.bfloat16)
        if i == 0:
            column_copy.wait()
        across = jnp.dot(misfit, column_scr[...], preferred_element_type=jnp.float32)
        across_out[angle, part] = across.astype(jnp.bfloat16)
        if i % FILTER_STEPS == FILTER_STEPS - 1:
            if angle == 0:
                slice_copy.wait()
            filter_rows(slice_scr, start_of, across_out[angle], outs, angle, rows)


def later_filter_kernel(rows, start_of, across_ref, slice_ref, *outs):
    for angle in range(across_ref.shape[0]):
        filter_rows(slice_ref, start_of, across_ref[angle], outs, angle, rows)


def tile_groups(count):
    group = next(g for g in (48, 32, 16, 8) if count % g == 0)
    return count // group, group


def start_tiles(tiles_ref, tile_scr, sems):
    count = tiles_ref.shape[0]
    groups, group = tile_groups(count)
    copies = []
    for g in range(groups):
        part = pl.ds(g * group, group)
        copies.append(pltpu.make_async_copy(tiles_ref.at[part], tile_scr.at[part], sems.at[g]))
    for copy in copies[:AHEAD]:
        copy.start()
    return copies


def tile_loop(live, copies, from_ref, to_ref, source, tiles, accs, held, dims):
    turns = (live + UNROLL - 1) // UNROLL

    def multiply(first):
        for u in range(UNROLL):
            held[u] = lax.dot_general(
                source[from_ref[first + u]], tiles[first + u], (dims, ((), ())),
                preferred_element_type=jnp.float32,
            )

    def accumulate(first):
        for u in range(UNROLL):
            place, into = to_ref[first + u], accs[u % len(accs)]
            into[place] = into[place] + held[u]

    def turn(i, carry):
        accumulate((i - 1) * UNROLL)
        multiply(i * UNROLL)
        return carry

    if copies is None:
        multiply(0)
        lax.fori_loop(1, turns, turn, 0)
    else:
        each = tiles.shape[0] // len(copies) // UNROLL
        for g, copy in enumerate(copies):
            copy.wait()
            if g + AHEAD < len(copies):
                copies[g + AHEAD].start()
            if g == 0:
                multiply(0)
            lax.fori_loop(max(1, g * each), jnp.minimum(turns, (g + 1) * each), turn, 0)
    accumulate((turns - 1) * UNROLL)


def back_kernel(live_ref, ray_ref, vox_ref, *refs):
    pieces = refs[:-9]
    tiles_ref, keep_out, send_out, ray_scr, tile_scr, acc, more, products, sems = refs[-9:]
    copies = start_tiles(tiles_ref, tile_scr, sems)
    acc[...] = jnp.zeros_like(acc)
    more[...] = jnp.zeros_like(more)
    held, _, columns = pieces[0].shape
    blocks = columns // LANES
    for m, piece in enumerate(pieces):
        for k in range(held):
            for b in range(blocks):
                ray_scr[(m * held + k) * blocks + b] = piece[k, :, b * LANES : (b + 1) * LANES]
    tile_loop(live_ref[0], copies, ray_ref, vox_ref, ray_scr, tile_scr, (acc, more), products, ((1,), (0,)))
    half = keep_out.shape[0]
    for i in range(half):
        keep_out[i] = (acc[i] + more[i]).astype(keep_out.dtype)
        send_out[i] = (acc[half + i] + more[half + i]).astype(send_out.dtype)


def fore_kernel(count, live_ref, vox_ref, ray_ref, *refs):
    pieces = refs[:count]
    tiles_ref = refs[count]
    outs = refs[count + 1 : -5]
    vox_scr, acc, more, products, vox_sems = refs[-5:]
    vox_copies = []
    first = 0
    for i, piece in enumerate(pieces):
        size = piece.shape[0]
        vox_copies.append(pltpu.make_async_copy(piece, vox_scr.at[pl.ds(first, size)], vox_sems.at[i]))
        first += size
    for copy in vox_copies:
        copy.start()
    acc[...] = jnp.zeros_like(acc)
    more[...] = jnp.zeros_like(more)
    for copy in vox_copies:
        copy.wait()
    tile_loop(live_ref[0], None, vox_ref, ray_ref, vox_scr, tiles_ref, (acc, more), products, ((1,), (1,)))
    held, _, columns = outs[0].shape
    blocks = columns // LANES
    for m, out in enumerate(outs):
        for k in range(held):
            for b in range(blocks):
                block = (m * held + k) * blocks + b
                out[k, :, b * LANES : (b + 1) * LANES] = (acc[block] + more[block]).astype(out.dtype)


def update_kernel(first, kept_ref, came_ref, volume_ref, new_out, vox_out):
    for j in range(kept_ref.shape[0]):
        lanes = slice(j * LANES, (j + 1) * LANES)
        grad = kept_ref[j].astype(jnp.float32) + came_ref[j].astype(jnp.float32)
        new = jnp.clip(volume_ref[first : first + kept_ref.shape[1], lanes] + step_size * grad, 0.0, 1.0)
        new_out[:, lanes] = new
        vox_out[j] = new.astype(vox_out.dtype)


def place_kernel(rows, count, start_of, *refs):
    pieces = refs[:count]
    out, sems = refs[-2:]
    copies = [
        pltpu.make_async_copy(
            piece, out.at[:, pl.ds(pl.multiple_of(start_of(m), 16), rows), :], sems.at[m]
        )
        for m, piece in enumerate(pieces)
    ]
    for copy in copies:
        copy.start()
    for copy in copies:
        copy.wait()


def add(a, b):
    return (a.astype(jnp.float32) + b.astype(jnp.float32)).astype(jnp.bfloat16)


def per_device(
    measured, predicted, slice_filter, column_filter, volume, tiles, tile_ray, tile_vox, live_tiles
):
    far_tiles = pltpu.with_memory_space_constraint(tiles, pltpu.HBM)
    bf16, f32, i32 = jnp.bfloat16, jnp.float32, jnp.int32
    held, _, columns = measured.shape
    angles, panels = lax.axis_size("angle"), lax.axis_size("panel")
    me_angle, me_panel = lax.axis_index("angle"), lax.axis_index("panel")
    rows_dev, vox_dev = volume.shape
    parts_rows = row_parts(rows_dev)
    offsets = [sum(parts_rows[:c]) for c in range(len(parts_rows))]
    chunks = len(parts_rows)
    blocks = columns // LANES
    ray_dev = held * blocks
    ray_blocks = ray_dev * angles
    block_dev = vox_dev // LANES
    vox_blocks = block_dev * panels
    slots = tiles.shape[0]
    bits = swap_bits(panels)

    rel = (tile_vox // block_dev) ^ me_panel
    order = (rel & 1) << (len(bits) - 1)
    for step in range(len(bits) - 1):
        mask = jnp.where((tile_vox // block_dev) % 2 == 0, swap_mask(0, step, bits), swap_mask(1, step, bits))
        order = order | (jnp.where((rel & mask) != 0, 1, 0) << (len(bits) - 2 - step))
    vox_place = order * block_dev + tile_vox % block_dev
    ray_place = ((tile_ray // ray_dev) ^ me_angle) * ray_dev + tile_ray % ray_dev
    dead = jnp.arange(slots, dtype=i32) >= live_tiles[0]
    vox_to = jnp.where(dead, vox_blocks, vox_place).astype(i32)
    ray_to = jnp.where(dead, ray_blocks, ray_place).astype(i32)


    def piece_shape(c):
        return jax.ShapeDtypeStruct((held, parts_rows[c], columns), bf16)

    def starts(c):
        return lambda m: (lax.axis_index("angle") ^ m) * rows_dev + offsets[c]

    def filtered(c, across):
        rows = parts_rows[c]
        if c == 0:
            return pl.pallas_call(
                functools.partial(first_filter_kernel, rows, starts(c)),
                out_shape=(jax.ShapeDtypeStruct(measured.shape, bf16),) + (piece_shape(c),) * angles,
                in_specs=[HBM_SPEC] * 4,
                out_specs=(VMEM_SPEC,) * (1 + angles),
                scratch_shapes=[
                    pltpu.VMEM(measured.shape, bf16),
                    pltpu.VMEM(predicted.shape, bf16),
                    pltpu.VMEM(slice_filter.shape, bf16),
                    pltpu.VMEM(column_filter.shape, bf16),
                    pltpu.SemaphoreType.DMA((2 * held * FILTER_STEPS + 2,)),
                ],
                compiler_params=params(58),
                cost_estimate=cost(7),
                name="first_filter",
            )(measured, predicted, slice_filter, column_filter)
        return (across,) + tuple(
            pl.pallas_call(
                functools.partial(later_filter_kernel, rows, starts(c)),
                out_shape=(piece_shape(c),) * angles,
                in_specs=[VMEM_SPEC] * 2,
                out_specs=(VMEM_SPEC,) * angles,
                compiler_params=params(20),
                cost_estimate=cost(2),
                name="later_filter",
            )(across, slice_filter)
        )

    tile_scratch = pltpu.VMEM(tiles.shape, bf16)
    tile_sems = pltpu.SemaphoreType.DMA((tile_groups(slots)[0],))

    def back(c, pieces):
        rows = parts_rows[c]
        half = jax.ShapeDtypeStruct((vox_blocks // 2, rows, LANES), bf16)
        return pl.pallas_call(
            back_kernel,
            out_shape=(half, half),
            in_specs=[SMEM_SPEC] * 3 + [VMEM_SPEC] * angles + [HBM_SPEC],
            out_specs=(VMEM_SPEC, VMEM_SPEC),
            scratch_shapes=[
                pltpu.VMEM((ray_blocks, rows, LANES), bf16),
                tile_scratch,
                pltpu.VMEM((vox_blocks + 1, rows, LANES), f32),
                pltpu.VMEM((vox_blocks + 1, rows, LANES), f32),
                pltpu.VMEM((UNROLL, rows, LANES), f32),
                tile_sems,
            ],
            compiler_params=params(26),
            cost_estimate=cost(6),
            name="back",
        )(live_tiles, ray_place, vox_to, *pieces, far_tiles)

    def fore(c, pieces):
        rows = parts_rows[c]
        return pl.pallas_call(
            functools.partial(fore_kernel, len(pieces)),
            out_shape=(piece_shape(c),) * angles,
            in_specs=[SMEM_SPEC] * 3 + [ANY_SPEC] * len(pieces) + [VMEM_SPEC],
            out_specs=(VMEM_SPEC,) * angles,
            scratch_shapes=[
                pltpu.VMEM((vox_blocks, rows, LANES), bf16),
                pltpu.VMEM((ray_blocks + 1, rows, LANES), f32),
                pltpu.VMEM((ray_blocks + 1, rows, LANES), f32),
                pltpu.VMEM((UNROLL, rows, LANES), f32),
                pltpu.SemaphoreType.DMA((len(pieces),)),
            ],
            compiler_params=params(26),
            cost_estimate=cost(8),
            name="fore",
        )(live_tiles, vox_place, ray_to, *pieces, tiles)

    def update(c, kept, came):
        rows = parts_rows[c]
        return pl.pallas_call(
            functools.partial(update_kernel, offsets[c]),
            out_shape=(
                jax.ShapeDtypeStruct((rows, vox_dev), f32),
                jax.ShapeDtypeStruct((block_dev, rows, LANES), bf16),
            ),
            in_specs=[VMEM_SPEC] * 3,
            out_specs=(VMEM_SPEC, VMEM_SPEC),
            compiler_params=params(20),
            cost_estimate=cost(1),
            name="update",
        )(kept, came, volume)

    def place(c, pieces, out):
        extra = () if out is None else (out,)
        return pl.pallas_call(
            functools.partial(place_kernel, parts_rows[c], angles, starts(c)),
            out_shape=jax.ShapeDtypeStruct(measured.shape, bf16),
            in_specs=[VMEM_SPEC] * angles + [ANY_SPEC] * len(extra),
            out_specs=ANY_SPEC,
            scratch_shapes=[pltpu.SemaphoreType.DMA((angles,))],
            input_output_aliases={angles: 0} if extra else {},
            compiler_params=params(20),
            cost_estimate=cost(1),
            name="place",
        )(*pieces, *extra)

    def spread(pieces):
        came = [pieces[0]]
        for m in range(1, angles):
            came.append(swap(pieces[m], "angle", m))
        return came

    across = None
    rays, new_parts, projected = [], [], []
    for c in range(chunks):
        across, *pieces = filtered(c, across)
        rays.append(spread(pieces))
    for c in range(chunks):
        kept, sent = back(c, rays[c])
        came = swap(sent, "panel", 1)
        half = kept.shape[0] // 2
        sent, kept = add(kept[half:], came[half:]), add(kept[:half], came[:half])
        for step in range(len(bits) - 1):
            came = swap_far(sent, step, bits)
            if step < len(bits) - 2:
                half = kept.shape[0] // 2
                sent, kept = add(kept[half:], came[half:]), add(kept[:half], came[:half])
        new_part, parts = update(c, kept, came)
        new_parts.append(new_part)
        for step in range(len(bits) - 2, -1, -1):
            came = swap_far(parts, step, bits)
            if step:
                parts = jnp.concatenate([parts, came], axis=0)
        pieces = [parts, came]
        for i in range(2):
            pieces.append(swap(pieces[i], "panel", 1))
        outs = fore(c, pieces)
        projected.append(spread(outs))
    out = None
    for c in range(chunks):
        out = place(c, projected[c], out)
    return (jnp.concatenate(new_parts, axis=0), out)


def solution(mesh):
    in_specs = (
        P(("angle", "panel"), None, None),
        P(("angle", "panel"), None, None),
        P(),
        P(),
        P("angle", "panel"),
        P("panel", None, None),
        P("panel"),
        P("panel"),
        P("panel"),
    )
    out_specs = (P("angle", "panel"), P(("angle", "panel"), None, None))
    return jax.shard_map(
        per_device, mesh=mesh, in_specs=in_specs, out_specs=out_specs, check_vma=False
    )
```

profile of v0, /device:TPU:0, one launch (start us, length us, event | category | flops | bytes accessed | tf_op | source)
XLA Modules:
  0.0 156.6 jit_solution(1183024955190556629)
XLA Ops:
  0.6 7.1 %first_filter.1 = (bf16[2,512,1024]{2,1,0:T(8,128)(2,1)}, bf16[2,64,1024]{2,1,0:T(8,128)(2,1)}, bf16[2,64,1024]{2,1,0:T(8,128)(2,1)}, bf16[2,64,1024]{2,1,0:T(8,128)(2,1)}, bf16[2,64,1024]{2,1,0:T(8,128)(2,1)}) custom-call(bf16[2,512,1024]{2,1,0:T(8,128)(2,1)} %measured.1, bf16[2,512,1024]{2,1,0:T(8,128)(2,1)} %predicted.1, bf16[512,512]{1,0:T(8,128)(2,1)} %slice_ref.3, ...), custom_call_target="tpu_custom_call" | custom-call | flops 7000000000 | tf_op jit(solution)/shard_map/first_filter/pallas_call | solution.py:276
  7.7 3.0 %collective-permute-start = (bf16[2,64,1024]{2,1,0:T(8,128)(2,1)}, bf16[2,64,1024]{2,1,0:T(8,128)(2,1)S(1)}, u32[]{:S(2)}, u32[]{:S(2)}) collective-permute-start(bf16[2,64,1024]{2,1,0:T(8,128)(2,1)} %get-tuple-element.28), channel_id=1, source_target_pairs={{0,8},{8,0},{16,24},{24,16},{1,9},{9,1},{17,25},{25,17},{2,10},{10... | collective-permute-start | bytes 786440 | tf_op jit(solution)/shard_map/ppermute | solution.py:57
  10.8 1.5 collective-permute-start.1
  12.3 1.6 %copy-done.2 = bf16[2,512,1024]{2,1,0:T(8,128)(2,1)S(1)} copy-done((bf16[2,512,1024]{2,1,0:T(8,128)(2,1)S(1)}, bf16[2,512,1024]{2,1,0:T(8,128)(2,1)}, u32[]{:S(2)}) %copy-start.2) | copy-done | bytes 2097176
  13.9 0.7 later_filter.1
  14.6 2.0 %collective-permute-start.6 = (bf16[2,64,1024]{2,1,0:T(8,128)(2,1)S(1)}, bf16[2,64,1024]{2,1,0:T(8,128)(2,1)S(1)}, u32[]{:S(2)}, u32[]{:S(2)}) collective-permute-start(bf16[2,64,1024]{2,1,0:T(8,128)(2,1)S(1)} %get-tuple-element.36), channel_id=1, source_target_pairs={{0,8},{8,0},{16,24},{24,16},{1,9},{9,1},{17,25},{25,17},{2,10},{10... | collective-permute-start | bytes 786440 | tf_op jit(solution)/shard_map/ppermute | solution.py:57
  16.6 1.5 collective-permute-start.7
  18.9 2.2 %collective-permute-start.8 = (bf16[2,64,1024]{2,1,0:T(8,128)(2,1)S(1)}, bf16[2,64,1024]{2,1,0:T(8,128)(2,1)S(1)}, u32[]{:S(2)}, u32[]{:S(2)}) collective-permute-start(bf16[2,64,1024]{2,1,0:T(8,128)(2,1)S(1)} %get-tuple-element.38), channel_id=1, source_target_pairs={{0,24},{8,16},{16,8},{24,0},{1,25},{9,17},{17,9},{25,1},{2,26},{10... | collective-permute-start | bytes 786440 | tf_op jit(solution)/shard_map/ppermute | solution.py:57
  21.1 4.4 %collective-permute-done.1.refs_2_ = bf16[2,64,1024]{2,1,0:T(8,128)(2,1)S(1)} collective-permute-done((bf16[2,64,1024]{2,1,0:T(8,128)(2,1)}, bf16[2,64,1024]{2,1,0:T(8,128)(2,1)S(1)}, u32[]{:S(2)}, u32[]{:S(2)}) %collective-permute-start.1) | collective-permute-done | bytes 262176 | tf_op jit(solution)/shard_map/ppermute | solution.py:57
  25.5 4.7 %back.2 = (bf16[64,64,128]{2,1,0:T(8,128)(2,1)S(1)}, bf16[64,64,128]{2,1,0:T(8,128)(2,1)S(1)}) custom-call(s32[1]{0:T(128)} %copy.15.live_ref, s32[192]{0:T(256)S(1)} %get-tuple-element.53.ray_ref, s32[192]{0:T(256)S(1)} %get-tuple-element.64.vox_ref, bf16[2,64,1024]{2,1,0:T(8,128)(2,1)S(1)} %copy-done.3, ...), custom_call_target="tpu_custom_call" | custom-call | flops 6000000000 | tf_op jit(solution)/shard_map/back/pallas_call | solution.py:310
  30.3 5.3 %collective-permute-done.7.refs_2_ = bf16[2,64,1024]{2,1,0:T(8,128)(2,1)S(1)} collective-permute-done((bf16[2,64,1024]{2,1,0:T(8,128)(2,1)S(1)}, bf16[2,64,1024]{2,1,0:T(8,128)(2,1)S(1)}, u32[]{:S(2)}, u32[]{:S(2)}) %collective-permute-start.7) | collective-permute-done | bytes 262176 | tf_op jit(solution)/shard_map/ppermute | solution.py:57
  35.6 4.9 %back.3 = (bf16[64,64,128]{2,1,0:T(8,128)(2,1)S(1)}, bf16[64,64,128]{2,1,0:T(8,128)(2,1)S(1)}) custom-call(s32[1]{0:T(128)} %copy.15.live_ref, s32[192]{0:T(256)S(1)} %get-tuple-element.53.ray_ref, s32[192]{0:T(256)S(1)} %get-tuple-element.64.vox_ref, bf16[2,64,1024]{2,1,0:T(8,128)(2,1)S(1)} %get-tuple-element.35.refs_0_, ...), custom_call_target="tpu_custom_call" | custom-call | flops 6000000000 | tf_op jit(solution)/shard_map/back/pallas_call | solution.py:310
  40.6 0.4 add_convert_fusion.3
  41.0 1.6 %collective-permute-start.4 = (bf16[32,64,128]{2,1,0:T(8,128)(2,1)S(1)}, bf16[32,64,128]{2,1,0:T(8,128)(2,1)S(1)}, u32[]{:S(2)}, u32[]{:S(2)}) collective-permute-start(bf16[32,64,128]{2,1,0:T(8,128)(2,1)S(1)} %get-tuple-element.57), channel_id=1, source_target_pairs={{0,2},{1,5},{2,0},{3,7},{4,6},{5,1},{6,4},{7,3},{8,10},{9,13},{10,... | collective-permute-start | bytes 1572872 | tf_op jit(solution)/shard_map/ppermute | solution.py:48
  42.7 0.6 collective-permute-done.9
  43.3 0.3 add_convert_fusion.1
  43.6 1.6 %collective-permute-start.10 = (bf16[32,64,128]{2,1,0:T(8,128)(2,1)S(1)}, bf16[32,64,128]{2,1,0:T(8,128)(2,1)S(1)}, u32[]{:S(2)}, u32[]{:S(2)}) collective-permute-start(bf16[32,64,128]{2,1,0:T(8,128)(2,1)S(1)} %get-tuple-element.59), channel_id=1, source_target_pairs={{0,2},{1,5},{2,0},{3,7},{4,6},{5,1},{6,4},{7,3},{8,10},{9,13},{10,... | collective-permute-start | bytes 1572872 | tf_op jit(solution)/shard_map/ppermute | solution.py:48
  45.2 11.0 %collective-permute-done.4 = bf16[32,64,128]{2,1,0:T(8,128)(2,1)S(1)} collective-permute-done((bf16[32,64,128]{2,1,0:T(8,128)(2,1)S(1)}, bf16[32,64,128]{2,1,0:T(8,128)(2,1)S(1)}, u32[]{:S(2)}, u32[]{:S(2)}) %collective-permute-start.4) | collective-permute-done | bytes 524320 | tf_op jit(solution)/shard_map/ppermute | solution.py:48
  56.3 0.2 add_convert_fusion.6
  56.5 1.8 %collective-permute-start.5 = (bf16[16,64,128]{2,1,0:T(8,128)(2,1)S(1)}, bf16[16,64,128]{2,1,0:T(8,128)(2,1)S(1)}, u32[]{:S(2)}, u32[]{:S(2)}) collective-permute-start(bf16[16,64,128]{2,1,0:T(8,128)(2,1)S(1)} %get-tuple-element.60), channel_id=1, source_target_pairs={{0,4},{1,3},{2,6},{3,1},{4,0},{5,7},{6,2},{7,5},{8,12},{9,11},{10,... | collective-permute-start | bytes 786440 | tf_op jit(solution)/shard_map/ppermute | solution.py:48
  58.3 13.6 %collective-permute-done.5.came_ref = bf16[16,64,128]{2,1,0:T(8,128)(2,1)S(1)} collective-permute-done((bf16[16,64,128]{2,1,0:T(8,128)(2,1)S(1)}, bf16[16,64,128]{2,1,0:T(8,128)(2,1)S(1)}, u32[]{:S(2)}, u32[]{:S(2)}) %collective-permute-start.5) | collective-permute-done | bytes 262176 | tf_op jit(solution)/shard_map/ppermute | solution.py:48
  71.9 0.1 update.2
  72.0 3.4 %collective-permute-start.19 = (bf16[16,64,128]{2,1,0:T(8,128)(2,1)S(1)}, bf16[16,64,128]{2,1,0:T(8,128)(2,1)S(1)}, u32[]{:S(2)}, u32[]{:S(2)}) collective-permute-start(bf16[16,64,128]{2,1,0:T(8,128)(2,1)S(1)} %get-tuple-element.47), channel_id=1, source_target_pairs={{0,4},{1,3},{2,6},{3,1},{4,0},{5,7},{6,2},{7,5},{8,12},{9,11},{10,... | collective-permute-start | bytes 786440 | tf_op jit(solution)/shard_map/ppermute | solution.py:48
  75.5 0.2 add_convert_fusion.4
  75.7 0.1 collective-permute-start.11
  75.8 6.4 %collective-permute-done.19 = bf16[16,64,128]{2,1,0:T(8,128)(2,1)S(1)} collective-permute-done((bf16[16,64,128]{2,1,0:T(8,128)(2,1)S(1)}, bf16[16,64,128]{2,1,0:T(8,128)(2,1)S(1)}, u32[]{:S(2)}, u32[]{:S(2)}) %collective-permute-start.19) | collective-permute-done | bytes 262176 | tf_op jit(solution)/shard_map/ppermute | solution.py:48
  82.2 2.9 %collective-permute-start.20 = (bf16[32,64,128]{2,1,0:T(8,128)(2,1)S(1)}, bf16[32,64,128]{2,1,0:T(8,128)(2,1)S(1)}, u32[]{:S(2)}, u32[]{:S(2)}) collective-permute-start(bf16[32,64,128]{2,1,0:T(8,128)(2,1)S(1)} %constant_dynamic-update-slice_fusion.2.refs_0_), channel_id=1, source_target_pairs={{0,2},{1,5},{2,0},{3,7},{4,6},{5,1},{6,4},{7,3},{8,10},{9,13},{10,... | collective-permute-start | bytes 1572872 | tf_op jit(solution)/shard_map/ppermute | solution.py:48
  85.1 6.9 %collective-permute-done.11.came_ref = bf16[16,64,128]{2,1,0:T(8,128)(2,1)S(1)} collective-permute-done((bf16[16,64,128]{2,1,0:T(8,128)(2,1)S(1)}, bf16[16,64,128]{2,1,0:T(8,128)(2,1)S(1)}, u32[]{:S(2)}, u32[]{:S(2)}) %collective-permute-start.11) | collective-permute-done | bytes 262176 | tf_op jit(solution)/shard_map/ppermute | solution.py:48
  92.0 0.1 update.3
  92.2 0.1 collective-permute-start.12
  92.3 13.0 %collective-permute-done.12 = bf16[16,64,128]{2,1,0:T(8,128)(2,1)S(1)} collective-permute-done((bf16[16,64,128]{2,1,0:T(8,128)(2,1)S(1)}, bf16[16,64,128]{2,1,0:T(8,128)(2,1)S(1)}, u32[]{:S(2)}, u32[]{:S(2)}) %collective-permute-start.12) | collective-permute-done | bytes 262176 | tf_op jit(solution)/shard_map/ppermute | solution.py:48
  105.3 6.7 %collective-permute-start.13 = (bf16[32,64,128]{2,1,0:T(8,128)(2,1)S(1)}, bf16[32,64,128]{2,1,0:T(8,128)(2,1)S(1)}, u32[]{:S(2)}, u32[]{:S(2)}) collective-permute-start(bf16[32,64,128]{2,1,0:T(8,128)(2,1)S(1)} %constant_dynamic-update-slice_fusion.refs_0_), channel_id=1, source_target_pairs={{0,2},{1,5},{2,0},{3,7},{4,6},{5,1},{6,4},{7,3},{8,10},{9,13},{10,... | collective-permute-start | bytes 1572872 | tf_op jit(solution)/shard_map/ppermute | solution.py:48
  111.9 0.5 collective-permute-start.22
  112.5 11.0 %collective-permute-done.13.refs_1_ = bf16[32,64,128]{2,1,0:T(8,128)(2,1)S(1)} collective-permute-done((bf16[32,64,128]{2,1,0:T(8,128)(2,1)S(1)}, bf16[32,64,128]{2,1,0:T(8,128)(2,1)S(1)}, u32[]{:S(2)}, u32[]{:S(2)}) %collective-permute-start.13) | collective-permute-done | bytes 524320 | tf_op jit(solution)/shard_map/ppermute | solution.py:48
  123.5 6.2 %fore.3 = (bf16[2,64,1024]{2,1,0:T(8,128)(2,1)S(1)}, bf16[2,64,1024]{2,1,0:T(8,128)(2,1)S(1)}, bf16[2,64,1024]{2,1,0:T(8,128)(2,1)S(1)}, bf16[2,64,1024]{2,1,0:T(8,128)(2,1)S(1)}) custom-call(s32[1]{0:T(128)} %copy.15.live_ref, s32[192]{0:T(256)S(1)} %get-tuple-element.65.vox_ref, s32[192]{0:T(256)S(1)} %get-tuple-element.52.ray_ref, ...), custom_call_target="tpu_custom_call" | custom-call | flops 8000000000 | tf_op jit(solution)/shard_map/fore/pallas_call | solution.py:330
  129.7 0.1 collective-permute-start.23
  129.8 2.1 %collective-permute-start.24 = (bf16[2,64,1024]{2,1,0:T(8,128)(2,1)S(1)}, bf16[2,64,1024]{2,1,0:T(8,128)(2,1)S(1)}, u32[]{:S(2)}, u32[]{:S(2)}) collective-permute-start(bf16[2,64,1024]{2,1,0:T(8,128)(2,1)S(1)} %get-tuple-element.50), channel_id=1, source_target_pairs={{0,16},{8,24},{16,0},{24,8},{1,17},{9,25},{17,1},{25,9},{2,18},{10... | collective-permute-start | bytes 786440 | tf_op jit(solution)/shard_map/ppermute | solution.py:57
  131.8 1.4 collective-permute-start.25
  133.2 6.2 %fore.2 = (bf16[2,64,1024]{2,1,0:T(8,128)(2,1)S(1)}, bf16[2,64,1024]{2,1,0:T(8,128)(2,1)S(1)}, bf16[2,64,1024]{2,1,0:T(8,128)(2,1)S(1)}, bf16[2,64,1024]{2,1,0:T(8,128)(2,1)S(1)}) custom-call(s32[1]{0:T(128)} %copy.15.live_ref, s32[192]{0:T(256)S(1)} %get-tuple-element.65.vox_ref, s32[192]{0:T(256)S(1)} %get-tuple-element.52.ray_ref, ...), custom_call_target="tpu_custom_call" | custom-call | flops 8000000000 | tf_op jit(solution)/shard_map/fore/pallas_call | solution.py:330
  139.4 0.1 collective-permute-start.16
  139.6 2.0 %collective-permute-start.17 = (bf16[2,64,1024]{2,1,0:T(8,128)(2,1)S(1)}, bf16[2,64,1024]{2,1,0:T(8,128)(2,1)S(1)}, u32[]{:S(2)}, u32[]{:S(2)}) collective-permute-start(bf16[2,64,1024]{2,1,0:T(8,128)(2,1)S(1)} %get-tuple-element.45), channel_id=1, source_target_pairs={{0,16},{8,24},{16,0},{24,8},{1,17},{9,25},{17,1},{25,9},{2,18},{10... | collective-permute-start | bytes 786440 | tf_op jit(solution)/shard_map/ppermute | solution.py:57
  141.6 1.4 collective-permute-start.18
  143.0 1.0 pad_maximum_fusion
  144.0 0.3 collective-permute-done.24.refs_2_
  144.4 1.0 place.2.refs_4_
  145.4 4.8 %collective-permute-done.16.refs_1_ = bf16[2,64,1024]{2,1,0:T(8,128)(2,1)S(1)} collective-permute-done((bf16[2,64,1024]{2,1,0:T(8,128)(2,1)S(1)}, bf16[2,64,1024]{2,1,0:T(8,128)(2,1)S(1)}, u32[]{:S(2)}, u32[]{:S(2)}) %collective-permute-start.16) | collective-permute-done | bytes 262176 | tf_op jit(solution)/shard_map/ppermute | solution.py:57
  150.2 5.2 %collective-permute-done.17.refs_2_ = bf16[2,64,1024]{2,1,0:T(8,128)(2,1)S(1)} collective-permute-done((bf16[2,64,1024]{2,1,0:T(8,128)(2,1)S(1)}, bf16[2,64,1024]{2,1,0:T(8,128)(2,1)S(1)}, u32[]{:S(2)}, u32[]{:S(2)}) %collective-permute-start.17) | collective-permute-done | bytes 262176 | tf_op jit(solution)/shard_map/ppermute | solution.py:57
  155.4 1.0 place.3
  (41 shorter events, 0.4 us)
Async XLA Ops:
  0.6 11.7 %copy-start.1 = (bf16[512,512]{1,0:T(8,128)(2,1)S(1)}, bf16[512,512]{1,0:T(8,128)(2,1)}, u32[]{:S(2)}) copy-start(bf16[512,512]{1,0:T(8,128)(2,1)} %slice_ref.3) | copy-start | bytes 1572868
  7.7 11.1 %collective-permute-start = (bf16[2,64,1024]{2,1,0:T(8,128)(2,1)}, bf16[2,64,1024]{2,1,0:T(8,128)(2,1)S(1)}, u32[]{:S(2)}, u32[]{:S(2)}) collective-permute-start(bf16[2,64,1024]{2,1,0:T(8,128)(2,1)} %get-tuple-element.28), channel_id=1, source_target_pairs={{0,8},{8,0},{16,24},{24,16},{1,9},{9,1},{17,25},{25,17},{2,10},{10... | collective-permute-start | bytes 786440 | tf_op jit(solution)/shard_map/ppermute | solution.py:57
  10.8 14.7 %collective-permute-start.1 = (bf16[2,64,1024]{2,1,0:T(8,128)(2,1)}, bf16[2,64,1024]{2,1,0:T(8,128)(2,1)S(1)}, u32[]{:S(2)}, u32[]{:S(2)}) collective-permute-start(bf16[2,64,1024]{2,1,0:T(8,128)(2,1)} %get-tuple-element.29), channel_id=1, source_target_pairs={{0,16},{8,24},{16,0},{24,8},{1,17},{9,25},{17,1},{25,9},{2,18},{10... | collective-permute-start | bytes 786440 | tf_op jit(solution)/shard_map/ppermute | solution.py:57
  12.3 13.2 %collective-permute-start.2 = (bf16[2,64,1024]{2,1,0:T(8,128)(2,1)}, bf16[2,64,1024]{2,1,0:T(8,128)(2,1)S(1)}, u32[]{:S(2)}, u32[]{:S(2)}) collective-permute-start(bf16[2,64,1024]{2,1,0:T(8,128)(2,1)} %get-tuple-element.30), channel_id=1, source_target_pairs={{0,24},{8,16},{16,8},{24,0},{1,25},{9,17},{17,9},{25,1},{2,26},{10... | collective-permute-start | bytes 786440 | tf_op jit(solution)/shard_map/ppermute | solution.py:57
  12.3 1.6 %copy-start.2 = (bf16[2,512,1024]{2,1,0:T(8,128)(2,1)S(1)}, bf16[2,512,1024]{2,1,0:T(8,128)(2,1)}, u32[]{:S(2)}) copy-start(bf16[2,512,1024]{2,1,0:T(8,128)(2,1)} %get-tuple-element.34.across_ref) | copy-start | bytes 6291460
  13.9 4.9 %copy-start.4 = (s32[192]{0:T(256)S(1)}, s32[192]{0:T(256)}, u32[]{:S(2)}) copy-start(s32[192]{0:T(256)} %param.15) | copy-start | bytes 2308
  13.9 4.9 %copy-start.5 = (s32[192]{0:T(256)S(1)}, s32[192]{0:T(256)}, u32[]{:S(2)}) copy-start(s32[192]{0:T(256)} %param.16) | copy-start | bytes 2308
  13.9 11.6 %copy-start.3 = (bf16[2,64,1024]{2,1,0:T(8,128)(2,1)S(1)}, bf16[2,64,1024]{2,1,0:T(8,128)(2,1)}, u32[]{:S(2)}) copy-start(bf16[2,64,1024]{2,1,0:T(8,128)(2,1)} %get-tuple-element.27.refs_0_) | copy-start | bytes 786436
  14.6 15.7 %collective-permute-start.6 = (bf16[2,64,1024]{2,1,0:T(8,128)(2,1)S(1)}, bf16[2,64,1024]{2,1,0:T(8,128)(2,1)S(1)}, u32[]{:S(2)}, u32[]{:S(2)}) collective-permute-start(bf16[2,64,1024]{2,1,0:T(8,128)(2,1)S(1)} %get-tuple-element.36), channel_id=1, source_target_pairs={{0,8},{8,0},{16,24},{24,16},{1,9},{9,1},{17,25},{25,17},{2,10},{10... | collective-permute-start | bytes 786440 | tf_op jit(solution)/shard_map/ppermute | solution.py:57
  16.6 19.0 %collective-permute-start.7 = (bf16[2,64,1024]{2,1,0:T(8,128)(2,1)S(1)}, bf16[2,64,1024]{2,1,0:T(8,128)(2,1)S(1)}, u32[]{:S(2)}, u32[]{:S(2)}) collective-permute-start(bf16[2,64,1024]{2,1,0:T(8,128)(2,1)S(1)} %get-tuple-element.37), channel_id=1, source_target_pairs={{0,16},{8,24},{16,0},{24,8},{1,17},{9,25},{17,1},{25,9},{2,18},{10... | collective-permute-start | bytes 786440 | tf_op jit(solution)/shard_map/ppermute | solution.py:57
  18.9 16.7 %collective-permute-start.8 = (bf16[2,64,1024]{2,1,0:T(8,128)(2,1)S(1)}, bf16[2,64,1024]{2,1,0:T(8,128)(2,1)S(1)}, u32[]{:S(2)}, u32[]{:S(2)}) collective-permute-start(bf16[2,64,1024]{2,1,0:T(8,128)(2,1)S(1)} %get-tuple-element.38), channel_id=1, source_target_pairs={{0,24},{8,16},{16,8},{24,0},{1,25},{9,17},{17,9},{25,1},{2,26},{10... | collective-permute-start | bytes 786440 | tf_op jit(solution)/shard_map/ppermute | solution.py:57
  30.2 10.4 %collective-permute-start.3 = (bf16[64,64,128]{2,1,0:T(8,128)(2,1)S(1)}, bf16[64,64,128]{2,1,0:T(8,128)(2,1)S(1)}, u32[]{:S(2)}, u32[]{:S(2)}) collective-permute-start(bf16[64,64,128]{2,1,0:T(8,128)(2,1)S(1)} %get-tuple-element.32), channel_id=1, source_target_pairs={{0,1},{1,0},{2,3},{3,2},{4,5},{5,4},{6,7},{7,6},{8,9},{9,8},{10,11... | collective-permute-start | bytes 3145736 | tf_op jit(solution)/shard_map/ppermute | solution.py:57
  40.5 2.7 %collective-permute-start.9 = (bf16[64,64,128]{2,1,0:T(8,128)(2,1)S(1)}, bf16[64,64,128]{2,1,0:T(8,128)(2,1)S(1)}, u32[]{:S(2)}, u32[]{:S(2)}) collective-permute-start(bf16[64,64,128]{2,1,0:T(8,128)(2,1)S(1)} %get-tuple-element.40), channel_id=1, source_target_pairs={{0,1},{1,0},{2,3},{3,2},{4,5},{5,4},{6,7},{7,6},{8,9},{9,8},{10,11... | collective-permute-start | bytes 3145736 | tf_op jit(solution)/shard_map/ppermute | solution.py:57
  40.6 31.3 %copy-start = (f32[128,2048]{1,0:T(8,128)S(1)}, f32[128,2048]{1,0:T(8,128)}, u32[]{:S(2)}) copy-start(f32[128,2048]{1,0:T(8,128)} %volume_ref.3) | copy-start | bytes 3145732
  41.0 15.2 %collective-permute-start.4 = (bf16[32,64,128]{2,1,0:T(8,128)(2,1)S(1)}, bf16[32,64,128]{2,1,0:T(8,128)(2,1)S(1)}, u32[]{:S(2)}, u32[]{:S(2)}) collective-permute-start(bf16[32,64,128]{2,1,0:T(8,128)(2,1)S(1)} %get-tuple-element.57), channel_id=1, source_target_pairs={{0,2},{1,5},{2,0},{3,7},{4,6},{5,1},{6,4},{7,3},{8,10},{9,13},{10,... | collective-permute-start | bytes 1572872 | tf_op jit(solution)/shard_map/ppermute | solution.py:48
  43.3 80.2 %slice-start = ((s8[6291456]{0:T(1024)(128)(4,1)}), s8[4194304]{0:T(1024)(128)(4,1)S(1)}, s32[]{:S(2)}) async-start(s8[6291456]{0:T(1024)(128)(4,1)} %bitcast.2), calls=%async_computation | async-start | bytes 8388608
  43.6 31.9 %collective-permute-start.10 = (bf16[32,64,128]{2,1,0:T(8,128)(2,1)S(1)}, bf16[32,64,128]{2,1,0:T(8,128)(2,1)S(1)}, u32[]{:S(2)}, u32[]{:S(2)}) collective-permute-start(bf16[32,64,128]{2,1,0:T(8,128)(2,1)S(1)} %get-tuple-element.59), channel_id=1, source_target_pairs={{0,2},{1,5},{2,0},{3,7},{4,6},{5,1},{6,4},{7,3},{8,10},{9,13},{10,... | collective-permute-start | bytes 1572872 | tf_op jit(solution)/shard_map/ppermute | solution.py:48
  56.5 15.5 %collective-permute-start.5 = (bf16[16,64,128]{2,1,0:T(8,128)(2,1)S(1)}, bf16[16,64,128]{2,1,0:T(8,128)(2,1)S(1)}, u32[]{:S(2)}, u32[]{:S(2)}) collective-permute-start(bf16[16,64,128]{2,1,0:T(8,128)(2,1)S(1)} %get-tuple-element.60), channel_id=1, source_target_pairs={{0,4},{1,3},{2,6},{3,1},{4,0},{5,7},{6,2},{7,5},{8,12},{9,11},{10,... | collective-permute-start | bytes 786440 | tf_op jit(solution)/shard_map/ppermute | solution.py:48
  71.9 51.5 %slice-start.1 = ((s8[6291456]{0:T(1024)(128)(4,1)}), s8[2097152]{0:T(1024)(128)(4,1)S(1)}, s32[]{:S(2)}) async-start(s8[6291456]{0:T(1024)(128)(4,1)} %bitcast.2), calls=%async_computation.1 | async-start | bytes 4194304
  72.0 10.1 %collective-permute-start.19 = (bf16[16,64,128]{2,1,0:T(8,128)(2,1)S(1)}, bf16[16,64,128]{2,1,0:T(8,128)(2,1)S(1)}, u32[]{:S(2)}, u32[]{:S(2)}) collective-permute-start(bf16[16,64,128]{2,1,0:T(8,128)(2,1)S(1)} %get-tuple-element.47), channel_id=1, source_target_pairs={{0,4},{1,3},{2,6},{3,1},{4,0},{5,7},{6,2},{7,5},{8,12},{9,11},{10,... | collective-permute-start | bytes 786440 | tf_op jit(solution)/shard_map/ppermute | solution.py:48
  75.7 16.4 %collective-permute-start.11 = (bf16[16,64,128]{2,1,0:T(8,128)(2,1)S(1)}, bf16[16,64,128]{2,1,0:T(8,128)(2,1)S(1)}, u32[]{:S(2)}, u32[]{:S(2)}) collective-permute-start(bf16[16,64,128]{2,1,0:T(8,128)(2,1)S(1)} %get-tuple-element.62), channel_id=1, source_target_pairs={{0,4},{1,3},{2,6},{3,1},{4,0},{5,7},{6,2},{7,5},{8,12},{9,11},{10,... | collective-permute-start | bytes 786440 | tf_op jit(solution)/shard_map/ppermute | solution.py:48
  82.2 29.7 %collective-permute-start.20 = (bf16[32,64,128]{2,1,0:T(8,128)(2,1)S(1)}, bf16[32,64,128]{2,1,0:T(8,128)(2,1)S(1)}, u32[]{:S(2)}, u32[]{:S(2)}) collective-permute-start(bf16[32,64,128]{2,1,0:T(8,128)(2,1)S(1)} %constant_dynamic-update-slice_fusion.2.refs_0_), channel_id=1, source_target_pairs={{0,2},{1,5},{2,0},{3,7},{4,6},{5,1},{6,4},{7,3},{8,10},{9,13},{10,... | collective-permute-start | bytes 1572872 | tf_op jit(solution)/shard_map/ppermute | solution.py:48
  92.2 13.1 %collective-permute-start.12 = (bf16[16,64,128]{2,1,0:T(8,128)(2,1)S(1)}, bf16[16,64,128]{2,1,0:T(8,128)(2,1)S(1)}, u32[]{:S(2)}, u32[]{:S(2)}) collective-permute-start(bf16[16,64,128]{2,1,0:T(8,128)(2,1)S(1)} %get-tuple-element.42), channel_id=1, source_target_pairs={{0,4},{1,3},{2,6},{3,1},{4,0},{5,7},{6,2},{7,5},{8,12},{9,11},{10,... | collective-permute-start | bytes 786440 | tf_op jit(solution)/shard_map/ppermute | solution.py:48
  105.3 18.2 %collective-permute-start.13 = (bf16[32,64,128]{2,1,0:T(8,128)(2,1)S(1)}, bf16[32,64,128]{2,1,0:T(8,128)(2,1)S(1)}, u32[]{:S(2)}, u32[]{:S(2)}) collective-permute-start(bf16[32,64,128]{2,1,0:T(8,128)(2,1)S(1)} %constant_dynamic-update-slice_fusion.refs_0_), channel_id=1, source_target_pairs={{0,2},{1,5},{2,0},{3,7},{4,6},{5,1},{6,4},{7,3},{8,10},{9,13},{10,... | collective-permute-start | bytes 1572872 | tf_op jit(solution)/shard_map/ppermute | solution.py:48
  111.9 11.5 %collective-permute-start.21 = (bf16[32,64,128]{2,1,0:T(8,128)(2,1)S(1)}, bf16[32,64,128]{2,1,0:T(8,128)(2,1)S(1)}, u32[]{:S(2)}, u32[]{:S(2)}) collective-permute-start(bf16[32,64,128]{2,1,0:T(8,128)(2,1)S(1)} %constant_dynamic-update-slice_fusion.2.refs_0_), channel_id=1, source_target_pairs={{0,1},{1,0},{2,3},{3,2},{4,5},{5,4},{6,7},{7,6},{8,9},{9,8},{10,11... | collective-permute-start | bytes 1572872 | tf_op jit(solution)/shard_map/ppermute | solution.py:57
  111.9 11.5 %collective-permute-start.22 = (bf16[32,64,128]{2,1,0:T(8,128)(2,1)S(1)}, bf16[32,64,128]{2,1,0:T(8,128)(2,1)S(1)}, u32[]{:S(2)}, u32[]{:S(2)}) collective-permute-start(bf16[32,64,128]{2,1,0:T(8,128)(2,1)S(1)} %collective-permute-done.20.refs_1_), channel_id=1, source_target_pairs={{0,1},{1,0},{2,3},{3,2},{4,5},{5,4},{6,7},{7,6},{8,9},{9,8},{10,11... | collective-permute-start | bytes 1572872 | tf_op jit(solution)/shard_map/ppermute | solution.py:57
  112.4 20.8 %collective-permute-start.14 = (bf16[32,64,128]{2,1,0:T(8,128)(2,1)S(1)}, bf16[32,64,128]{2,1,0:T(8,128)(2,1)S(1)}, u32[]{:S(2)}, u32[]{:S(2)}) collective-permute-start(bf16[32,64,128]{2,1,0:T(8,128)(2,1)S(1)} %constant_dynamic-update-slice_fusion.refs_0_), channel_id=1, source_target_pairs={{0,1},{1,0},{2,3},{3,2},{4,5},{5,4},{6,7},{7,6},{8,9},{9,8},{10,11... | collective-permute-start | bytes 1572872 | tf_op jit(solution)/shard_map/ppermute | solution.py:57
  123.4 9.8 %collective-permute-start.15 = (bf16[32,64,128]{2,1,0:T(8,128)(2,1)S(1)}, bf16[32,64,128]{2,1,0:T(8,128)(2,1)S(1)}, u32[]{:S(2)}, u32[]{:S(2)}) collective-permute-start(bf16[32,64,128]{2,1,0:T(8,128)(2,1)S(1)} %collective-permute-done.13.refs_1_), channel_id=1, source_target_pairs={{0,1},{1,0},{2,3},{3,2},{4,5},{5,4},{6,7},{7,6},{8,9},{9,8},{10,11... | collective-permute-start | bytes 1572872 | tf_op jit(solution)/shard_map/ppermute | solution.py:57
  129.7 11.9 %collective-permute-start.23 = (bf16[2,64,1024]{2,1,0:T(8,128)(2,1)S(1)}, bf16[2,64,1024]{2,1,0:T(8,128)(2,1)S(1)}, u32[]{:S(2)}, u32[]{:S(2)}) collective-permute-start(bf16[2,64,1024]{2,1,0:T(8,128)(2,1)S(1)} %get-tuple-element.49), channel_id=1, source_target_pairs={{0,8},{8,0},{16,24},{24,16},{1,9},{9,1},{17,25},{25,17},{2,10},{10... | collective-permute-start | bytes 786440 | tf_op jit(solution)/shard_map/ppermute | solution.py:57
  129.8 14.6 %collective-permute-start.24 = (bf16[2,64,1024]{2,1,0:T(8,128)(2,1)S(1)}, bf16[2,64,1024]{2,1,0:T(8,128)(2,1)S(1)}, u32[]{:S(2)}, u32[]{:S(2)}) collective-permute-start(bf16[2,64,1024]{2,1,0:T(8,128)(2,1)S(1)} %get-tuple-element.50), channel_id=1, source_target_pairs={{0,16},{8,24},{16,0},{24,8},{1,17},{9,25},{17,1},{25,9},{2,18},{10... | collective-permute-start | bytes 786440 | tf_op jit(solution)/shard_map/ppermute | solution.py:57
  131.8 12.6 %collective-permute-start.25 = (bf16[2,64,1024]{2,1,0:T(8,128)(2,1)S(1)}, bf16[2,64,1024]{2,1,0:T(8,128)(2,1)S(1)}, u32[]{:S(2)}, u32[]{:S(2)}) collective-permute-start(bf16[2,64,1024]{2,1,0:T(8,128)(2,1)S(1)} %get-tuple-element.51), channel_id=1, source_target_pairs={{0,24},{8,16},{16,8},{24,0},{1,25},{9,17},{17,9},{25,1},{2,26},{10... | collective-permute-start | bytes 786440 | tf_op jit(solution)/shard_map/ppermute | solution.py:57
  139.4 10.8 %collective-permute-start.16 = (bf16[2,64,1024]{2,1,0:T(8,128)(2,1)S(1)}, bf16[2,64,1024]{2,1,0:T(8,128)(2,1)S(1)}, u32[]{:S(2)}, u32[]{:S(2)}) collective-permute-start(bf16[2,64,1024]{2,1,0:T(8,128)(2,1)S(1)} %get-tuple-element.44), channel_id=1, source_target_pairs={{0,8},{8,0},{16,24},{24,16},{1,9},{9,1},{17,25},{25,17},{2,10},{10... | collective-permute-start | bytes 786440 | tf_op jit(solution)/shard_map/ppermute | solution.py:57
  139.6 15.8 %collective-permute-start.17 = (bf16[2,64,1024]{2,1,0:T(8,128)(2,1)S(1)}, bf16[2,64,1024]{2,1,0:T(8,128)(2,1)S(1)}, u32[]{:S(2)}, u32[]{:S(2)}) collective-permute-start(bf16[2,64,1024]{2,1,0:T(8,128)(2,1)S(1)} %get-tuple-element.45), channel_id=1, source_target_pairs={{0,16},{8,24},{16,0},{24,8},{1,17},{9,25},{17,1},{25,9},{2,18},{10... | collective-permute-start | bytes 786440 | tf_op jit(solution)/shard_map/ppermute | solution.py:57
  141.6 13.8 %collective-permute-start.18 = (bf16[2,64,1024]{2,1,0:T(8,128)(2,1)S(1)}, bf16[2,64,1024]{2,1,0:T(8,128)(2,1)S(1)}, u32[]{:S(2)}, u32[]{:S(2)}) collective-permute-start(bf16[2,64,1024]{2,1,0:T(8,128)(2,1)S(1)} %get-tuple-element.46), channel_id=1, source_target_pairs={{0,24},{8,16},{16,8},{24,0},{1,25},{9,17},{17,9},{25,1},{2,26},{10... | collective-permute-start | bytes 786440 | tf_op jit(solution)/shard_map/ppermute | solution.py:57
where the time goes:
time: 157 us
  waiting for transfers between devices  82.5 us (53%)
  starting transfers between devices  36.4 us (23%)
  Pallas kernels  32.1 us (20%)
  other arithmetic  2.17 us (1%)
  local copies, waits for them, and re-layouts  1.73 us (1%)
  between operations  1.69 us (1%)
    ppermute x8, waiting for transfers between devices, swap_far(): lax.ppermute(value, 'panel', [(i, i ^ swap_mask(i, step, bits)) for i in...  61.9 us
    ppermute x18, waiting for transfers between devices, swap(): return lax.ppermute(value, axis, [(i, i ^ mask) for i in range(size)])  20.6 us
    ppermute x8, starting transfers between devices, swap_far(): lax.ppermute(value, 'panel', [(i, i ^ swap_mask(i, step, bits)) for i in...  18.3 us
    ppermute x18, starting transfers between devices, swap(): return lax.ppermute(value, axis, [(i, i ^ mask) for i in range(size)])  18.1 us
    pallas_call x2, Pallas kernels, fore(): pl.pallas_call(functools.partial(fore_kernel, len(pieces)), out_shape=(pi...  12.4 us
    pallas_call x2, Pallas kernels, back(): pl.pallas_call(back_kernel, out_shape=(half, half), in_specs=[SMEM_SPEC]...  9.67 us
    pallas_call x1, Pallas kernels, filtered(): pl.pallas_call(functools.partial(first_filter_kernel, rows, starts(c)), o...  7.08 us
  transfers between devices with their start and end apart: 26, of which 12 were waited for; matrix products, arithmetic and copies ran while one was open for 1% of the time, Pallas kernels for 15%

commit v1 on v0

--- a/solution.py
+++ b/solution.py
@@ -13,7 +13,7 @@
 UNROLL = 48
 AHEAD = 4
 FILTER_STEPS = 2
-CUTS = (1, 1)
+CUTS = (2, 4, 2)
 MIB = 1024 * 1024
 
 
@@ -101,9 +101,11 @@
             filter_rows(slice_scr, start_of, across_out[angle], outs, angle, rows)
 
 
-def later_filter_kernel(rows, start_of, across_ref, slice_ref, *outs):
-    for angle in range(across_ref.shape[0]):
-        filter_rows(slice_ref, start_of, across_ref[angle], outs, angle, rows)
+def later_filter_kernel(rows, starts, across_ref, slice_ref, *outs):
+    each = len(outs) // len(rows)
+    for c in range(len(rows)):
+        for angle in range(across_ref.shape[0]):
+            filter_rows(slice_ref, starts[c], across_ref[angle], outs[c * each : (c + 1) * each], angle, rows[c])
 
 
 def tile_groups(count):
@@ -270,36 +272,36 @@
     def starts(c):
         return lambda m: (lax.axis_index("angle") ^ m) * rows_dev + offsets[c]
 
-    def filtered(c, across):
-        rows = parts_rows[c]
-        if c == 0:
-            return pl.pallas_call(
-                functools.partial(first_filter_kernel, rows, starts(c)),
-                out_shape=(jax.ShapeDtypeStruct(measured.shape, bf16),) + (piece_shape(c),) * angles,
-                in_specs=[HBM_SPEC] * 4,
-                out_specs=(VMEM_SPEC,) * (1 + angles),
-                scratch_shapes=[
-                    pltpu.VMEM(measured.shape, bf16),
-                    pltpu.VMEM(predicted.shape, bf16),
-                    pltpu.VMEM(slice_filter.shape, bf16),
-                    pltpu.VMEM(column_filter.shape, bf16),
-                    pltpu.SemaphoreType.DMA((2 * held * FILTER_STEPS + 2,)),
-                ],
-                compiler_params=params(58),
-                cost_estimate=cost(7),
-                name="first_filter",
-            )(measured, predicted, slice_filter, column_filter)
-        return (across,) + tuple(
-            pl.pallas_call(
-                functools.partial(later_filter_kernel, rows, starts(c)),
-                out_shape=(piece_shape(c),) * angles,
-                in_specs=[VMEM_SPEC] * 2,
-                out_specs=(VMEM_SPEC,) * angles,
-                compiler_params=params(20),
-                cost_estimate=cost(2),
-                name="later_filter",
-            )(across, slice_filter)
-        )
+    def first_filtered():
+        return pl.pallas_call(
+            functools.partial(first_filter_kernel, parts_rows[0], starts(0)),
+            out_shape=(jax.ShapeDtypeStruct(measured.shape, bf16),) + (piece_shape(0),) * angles,
+            in_specs=[HBM_SPEC] * 4,
+            out_specs=(VMEM_SPEC,) * (1 + angles),
+            scratch_shapes=[
+                pltpu.VMEM(measured.shape, bf16),
+                pltpu.VMEM(predicted.shape, bf16),
+                pltpu.VMEM(slice_filter.shape, bf16),
+                pltpu.VMEM(column_filter.shape, bf16),
+                pltpu.SemaphoreType.DMA((2 * held * FILTER_STEPS + 2,)),
+            ],
+            compiler_params=params(58),
+            cost_estimate=cost(7),
+            name="first_filter",
+        )(measured, predicted, slice_filter, column_filter)
+
+    def later_filtered(across):
+        later = range(1, chunks)
+        outs = pl.pallas_call(
+            functools.partial(later_filter_kernel, parts_rows[1:], [starts(c) for c in later]),
+            out_shape=tuple(piece_shape(c) for c in later for _ in range(angles)),
+            in_specs=[VMEM_SPEC] * 2,
+            out_specs=(VMEM_SPEC,) * (len(later) * angles),
+            compiler_params=params(20),
+            cost_estimate=cost(2),
+            name="later_filter",
+        )(across, slice_filter)
+        return [outs[c * angles : (c + 1) * angles] for c in range(len(later))]
 
     tile_scratch = pltpu.VMEM(tiles.shape, bf16)
     tile_sems = pltpu.SemaphoreType.DMA((tile_groups(slots)[0],))
@@ -379,11 +381,12 @@
             came.append(swap(pieces[m], "angle", m))
         return came
 
-    across = None
-    rays, new_parts, projected = [], [], []
-    for c in range(chunks):
-        across, *pieces = filtered(c, across)
-        rays.append(spread(pieces))
+    new_parts, projected = [], []
+    across, *pieces = first_filtered()
+    rays = [spread(pieces)]
+    if chunks > 1:
+        later = later_filtered(across)
+        rays += [spread(later[c - 1]) for c in range(1, chunks)]
     for c in range(chunks):
         kept, sent = back(c, rays[c])
         came = swap(sent, "panel", 1)
@@ -408,7 +411,8 @@
     out = None
     for c in range(chunks):
         out = place(c, projected[c], out)
-    return (jnp.concatenate(new_parts, axis=0), out)
+    new_volume = jnp.concatenate(new_parts, axis=0)
+    return (new_volume, out)
 
 
 def solution(mesh):

time: 157 us -> 164 us (1.045)
  waiting for transfers between devices: 82.5 us -> 65.7 us
  starting transfers between devices: 36.4 us -> 51.9 us
  Pallas kernels: 32.1 us -> 40.3 us
    ppermute x8 -> x12, waiting for transfers between devices: 61.9 us -> 47.6 us  [swap_far(): lax.ppermute(value, 'panel', [(i, i ^ swap_mask(i, step, bits)) for i in...]
    ppermute x18 -> x27, starting transfers between devices: 18.1 us -> 27.7 us  [swap(): return lax.ppermute(value, axis, [(i, i ^ mask) for i in range(size)])]
    ppermute x8 -> x12, starting transfers between devices: 18.3 us -> 24.1 us  [swap_far(): lax.ppermute(value, 'panel', [(i, i ^ swap_mask(i, step, bits)) for i in...]
    pallas_call x2 -> x3, Pallas kernels: 9.67 us -> 13.8 us  [back(): pl.pallas_call(back_kernel, out_shape=(half, half), in_specs=[SMEM_SPEC]...]
    pallas_call x2 -> x3, Pallas kernels: 12.4 us -> 15.8 us  [fore(): pl.pallas_call(functools.partial(fore_kernel, len(pieces)), out_shape=(pi...]
    ppermute x18 -> x27, waiting for transfers between devices: 20.6 us -> 18.1 us  [swap(): return lax.ppermute(value, axis, [(i, i ^ mask) for i in range(size)])]
  transfers between devices with their start and end apart: 26 -> 39, of which waited for: 12 -> 10; matrix products, arithmetic and copies ran while one was open for 1% -> 1% of each run, Pallas kernels for 15% -> 19%
where the time goes in v1:
time: 164 us; the launch traced here: 163 us
  waiting for transfers between devices  65.7 us (40%)
  starting transfers between devices  51.9 us (32%)
  Pallas kernels  40.3 us (25%)
  other arithmetic  2.07 us (1%)
  between operations  1.78 us (1%)
  local copies, waits for them, and re-layouts  1.74 us (1%)
    ppermute x12, waiting for transfers between devices, swap_far(): lax.ppermute(value, 'panel', [(i, i ^ swap_mask(i, step, bits)) for i in...  47.6 us
    ppermute x27, starting transfers between devices, swap(): return lax.ppermute(value, axis, [(i, i ^ mask) for i in range(size)])  27.7 us
    ppermute x12, starting transfers between devices, swap_far(): lax.ppermute(value, 'panel', [(i, i ^ swap_mask(i, step, bits)) for i in...  24.1 us
    ppermute x27, waiting for transfers between devices, swap(): return lax.ppermute(value, axis, [(i, i ^ mask) for i in range(size)])  18.1 us
    pallas_call x3, Pallas kernels, fore(): pl.pallas_call(functools.partial(fore_kernel, len(pieces)), out_shape=(pi...  15.8 us
    pallas_call x3, Pallas kernels, back(): pl.pallas_call(back_kernel, out_shape=(half, half), in_specs=[SMEM_SPEC]...  13.8 us
    pallas_call x1, Pallas kernels, first_filtered(): pl.pallas_call(functools.partial(first_filter_kernel, parts_rows[0], star...  6.75 us
  transfers between devices with their start and end apart: 39, of which 10 were waited for; matrix products, arithmetic and copies ran while one was open for 1% of the time, Pallas kernels for 19%

profile of v1, /device:TPU:0, one launch (start us, length us, event | category | flops | bytes accessed | tf_op | source)
XLA Modules:
  0.0 163.4 jit_solution(9909431924258187089)
XLA Ops:
  0.6 6.7 %first_filter.1 = (bf16[2,512,1024]{2,1,0:T(8,128)(2,1)}, bf16[2,32,1024]{2,1,0:T(8,128)(2,1)}, bf16[2,32,1024]{2,1,0:T(8,128)(2,1)}, bf16[2,32,1024]{2,1,0:T(8,128)(2,1)}, bf16[2,32,1024]{2,1,0:T(8,128)(2,1)}) custom-call(bf16[2,512,1024]{2,1,0:T(8,128)(2,1)} %measured.1, bf16[2,512,1024]{2,1,0:T(8,128)(2,1)} %predicted.1, bf16[512,512]{1,0:T(8,128)(2,1)} %slice_ref.3, ...), custom_call_target="tpu_custom_call" | custom-call | flops 7000000000 | tf_op jit(solution)/shard_map/first_filter/pallas_call | solution.py:276
  7.4 1.6 copy-done.2
  9.0 1.0 later_filter.1
  10.0 3.0 %collective-permute-start.6 = (bf16[2,64,1024]{2,1,0:T(8,128)(2,1)S(1)}, bf16[2,64,1024]{2,1,0:T(8,128)(2,1)S(1)}, u32[]{:S(2)}, u32[]{:S(2)}) collective-permute-start(bf16[2,64,1024]{2,1,0:T(8,128)(2,1)S(1)} %get-tuple-element.48), channel_id=1, source_target_pairs={{0,8},{8,0},{16,24},{24,16},{1,9},{9,1},{17,25},{25,17},{2,10},{10... | collective-permute-start | bytes 786440 | tf_op jit(solution)/shard_map/ppermute | solution.py:57
  13.1 1.5 collective-permute-start.7
  14.6 1.9 %collective-permute-start = (bf16[2,32,1024]{2,1,0:T(8,128)(2,1)S(1)}, bf16[2,32,1024]{2,1,0:T(8,128)(2,1)S(1)}, u32[]{:S(2)}, u32[]{:S(2)}) collective-permute-start(bf16[2,32,1024]{2,1,0:T(8,128)(2,1)S(1)} %copy-done.8), channel_id=1, source_target_pairs={{0,8},{8,0},{16,24},{24,16},{1,9},{9,1},{17,25},{25,17},{2,10},{10... | collective-permute-start | bytes 393224 | tf_op jit(solution)/shard_map/ppermute | solution.py:57
  16.5 1.5 collective-permute-start.1
  18.8 1.4 collective-permute-done.6.refs_1_
  20.2 3.0 %collective-permute-start.2 = (bf16[2,32,1024]{2,1,0:T(8,128)(2,1)S(1)}, bf16[2,32,1024]{2,1,0:T(8,128)(2,1)S(1)}, u32[]{:S(2)}, u32[]{:S(2)}) collective-permute-start(bf16[2,32,1024]{2,1,0:T(8,128)(2,1)S(1)} %copy-done.6), channel_id=1, source_target_pairs={{0,24},{8,16},{16,8},{24,0},{1,25},{9,17},{17,9},{25,1},{2,26},{10... | collective-permute-start | bytes 393224 | tf_op jit(solution)/shard_map/ppermute | solution.py:57
  23.2 4.6 %collective-permute-done.7.refs_2_ = bf16[2,64,1024]{2,1,0:T(8,128)(2,1)S(1)} collective-permute-done((bf16[2,64,1024]{2,1,0:T(8,128)(2,1)S(1)}, bf16[2,64,1024]{2,1,0:T(8,128)(2,1)S(1)}, u32[]{:S(2)}, u32[]{:S(2)}) %collective-permute-start.7) | collective-permute-done | bytes 262176 | tf_op jit(solution)/shard_map/ppermute | solution.py:57
  27.9 2.4 %collective-permute-start.13 = (bf16[2,32,1024]{2,1,0:T(8,128)(2,1)S(1)}, bf16[2,32,1024]{2,1,0:T(8,128)(2,1)S(1)}, u32[]{:S(2)}, u32[]{:S(2)}) collective-permute-start(bf16[2,32,1024]{2,1,0:T(8,128)(2,1)S(1)} %get-tuple-element.56), channel_id=1, source_target_pairs={{0,16},{8,24},{16,0},{24,8},{1,17},{9,25},{17,1},{25,9},{2,18},{10... | collective-permute-start | bytes 393224 | tf_op jit(solution)/shard_map/ppermute | solution.py:57
  30.2 4.7 %back.4 = (bf16[64,64,128]{2,1,0:T(8,128)(2,1)S(1)}, bf16[64,64,128]{2,1,0:T(8,128)(2,1)S(1)}) custom-call(s32[1]{0:T(128)} %copy.18.live_ref, s32[192]{0:T(256)S(1)} %get-tuple-element.77.ray_ref, s32[192]{0:T(256)S(1)} %get-tuple-element.92.vox_ref, bf16[2,64,1024]{2,1,0:T(8,128)(2,1)S(1)} %get-tuple-element.47.refs_0_, ...), custom_call_target="tpu_custom_call" | custom-call | flops 6000000000 | tf_op jit(solution)/shard_map/back/pallas_call | solution.py:312
  35.0 1.5 collective-permute-start.14
  36.6 4.5 %back.3 = (bf16[64,32,128]{2,1,0:T(8,128)(2,1)S(1)}, bf16[64,32,128]{2,1,0:T(8,128)(2,1)S(1)}) custom-call(s32[1]{0:T(128)} %copy.18.live_ref, s32[192]{0:T(256)S(1)} %get-tuple-element.77.ray_ref, s32[192]{0:T(256)S(1)} %get-tuple-element.92.vox_ref, bf16[2,32,1024]{2,1,0:T(8,128)(2,1)S(1)} %copy-done.3, ...), custom_call_target="tpu_custom_call" | custom-call | flops 6000000000 | tf_op jit(solution)/shard_map/back/pallas_call | solution.py:312
  41.0 0.6 collective-permute-start.3
  41.6 4.6 %back.5 = (bf16[64,32,128]{2,1,0:T(8,128)(2,1)S(1)}, bf16[64,32,128]{2,1,0:T(8,128)(2,1)S(1)}) custom-call(s32[1]{0:T(128)} %copy.18.live_ref, s32[192]{0:T(256)S(1)} %get-tuple-element.77.ray_ref, s32[192]{0:T(256)S(1)} %get-tuple-element.92.vox_ref, bf16[2,32,1024]{2,1,0:T(8,128)(2,1)S(1)} %get-tuple-element.54.refs_0_, ...), custom_call_target="tpu_custom_call" | custom-call | flops 6000000000 | tf_op jit(solution)/shard_map/back/pallas_call | solution.py:312
  46.8 1.2 collective-permute-start.10
  48.2 0.9 collective-permute-start.4
  49.2 1.2 collective-permute-start.16
  50.5 16.6 %collective-permute-done.4 = bf16[32,32,128]{2,1,0:T(8,128)(2,1)S(1)} collective-permute-done((bf16[32,32,128]{2,1,0:T(8,128)(2,1)S(1)}, bf16[32,32,128]{2,1,0:T(8,128)(2,1)S(1)}, u32[]{:S(2)}, u32[]{:S(2)}) %collective-permute-start.4) | collective-permute-done | bytes 262176 | tf_op jit(solution)/shard_map/ppermute | solution.py:48
  67.1 2.3 %collective-permute-start.5 = (bf16[16,32,128]{2,1,0:T(8,128)(2,1)S(1)}, bf16[16,32,128]{2,1,0:T(8,128)(2,1)S(1)}, u32[]{:S(2)}, u32[]{:S(2)}) collective-permute-start(bf16[16,32,128]{2,1,0:T(8,128)(2,1)S(1)} %get-tuple-element.88), channel_id=1, source_target_pairs={{0,4},{1,3},{2,6},{3,1},{4,0},{5,7},{6,2},{7,5},{8,12},{9,11},{10,... | collective-permute-start | bytes 393224 | tf_op jit(solution)/shard_map/ppermute | solution.py:48
  69.6 0.7 collective-permute-start.11
  70.4 5.9 %collective-permute-done.16 = bf16[32,32,128]{2,1,0:T(8,128)(2,1)S(1)} collective-permute-done((bf16[32,32,128]{2,1,0:T(8,128)(2,1)S(1)}, bf16[32,32,128]{2,1,0:T(8,128)(2,1)S(1)}, u32[]{:S(2)}, u32[]{:S(2)}) %collective-permute-start.16) | collective-permute-done | bytes 262176 | tf_op jit(solution)/shard_map/ppermute | solution.py:48
  76.5 3.0 %collective-permute-start.32 = (bf16[16,32,128]{2,1,0:T(8,128)(2,1)S(1)}, bf16[16,32,128]{2,1,0:T(8,128)(2,1)S(1)}, u32[]{:S(2)}, u32[]{:S(2)}) collective-permute-start(bf16[16,32,128]{2,1,0:T(8,128)(2,1)S(1)} %get-tuple-element.71), channel_id=1, source_target_pairs={{0,4},{1,3},{2,6},{3,1},{4,0},{5,7},{6,2},{7,5},{8,12},{9,11},{10,... | collective-permute-start | bytes 393224 | tf_op jit(solution)/shard_map/ppermute | solution.py:48
  79.5 1.1 collective-permute-done.11.came_ref
  80.7 2.9 %collective-permute-start.25 = (bf16[16,64,128]{2,1,0:T(8,128)(2,1)S(1)}, bf16[16,64,128]{2,1,0:T(8,128)(2,1)S(1)}, u32[]{:S(2)}, u32[]{:S(2)}) collective-permute-start(bf16[16,64,128]{2,1,0:T(8,128)(2,1)S(1)} %get-tuple-element.66), channel_id=1, source_target_pairs={{0,4},{1,3},{2,6},{3,1},{4,0},{5,7},{6,2},{7,5},{8,12},{9,11},{10,... | collective-permute-start | bytes 786440 | tf_op jit(solution)/shard_map/ppermute | solution.py:48
  83.6 2.9 %collective-permute-done.32 = bf16[16,32,128]{2,1,0:T(8,128)(2,1)S(1)} collective-permute-done((bf16[16,32,128]{2,1,0:T(8,128)(2,1)S(1)}, bf16[16,32,128]{2,1,0:T(8,128)(2,1)S(1)}, u32[]{:S(2)}, u32[]{:S(2)}) %collective-permute-start.32) | collective-permute-done | bytes 131104 | tf_op jit(solution)/shard_map/ppermute | solution.py:48
  86.5 2.6 %collective-permute-start.33 = (bf16[32,32,128]{2,1,0:T(8,128)(2,1)S(1)}, bf16[32,32,128]{2,1,0:T(8,128)(2,1)S(1)}, u32[]{:S(2)}, u32[]{:S(2)}) collective-permute-start(bf16[32,32,128]{2,1,0:T(8,128)(2,1)S(1)} %constant_dynamic-update-slice_fusion.4.refs_0_), channel_id=1, source_target_pairs={{0,2},{1,5},{2,0},{3,7},{4,6},{5,1},{6,4},{7,3},{8,10},{9,13},{10,... | collective-permute-start | bytes 786440 | tf_op jit(solution)/shard_map/ppermute | solution.py:48
  89.1 4.0 %collective-permute-done.25 = bf16[16,64,128]{2,1,0:T(8,128)(2,1)S(1)} collective-permute-done((bf16[16,64,128]{2,1,0:T(8,128)(2,1)S(1)}, bf16[16,64,128]{2,1,0:T(8,128)(2,1)S(1)}, u32[]{:S(2)}, u32[]{:S(2)}) %collective-permute-start.25) | collective-permute-done | bytes 262176 | tf_op jit(solution)/shard_map/ppermute | solution.py:48
  93.1 2.2 %collective-permute-start.26 = (bf16[32,64,128]{2,1,0:T(8,128)(2,1)S(1)}, bf16[32,64,128]{2,1,0:T(8,128)(2,1)S(1)}, u32[]{:S(2)}, u32[]{:S(2)}) collective-permute-start(bf16[32,64,128]{2,1,0:T(8,128)(2,1)S(1)} %constant_dynamic-update-slice_fusion.2.refs_0_), channel_id=1, source_target_pairs={{0,2},{1,5},{2,0},{3,7},{4,6},{5,1},{6,4},{7,3},{8,10},{9,13},{10,... | collective-permute-start | bytes 1572872 | tf_op jit(solution)/shard_map/ppermute | solution.py:48
  95.4 3.9 %collective-permute-start.18 = (bf16[16,32,128]{2,1,0:T(8,128)(2,1)S(1)}, bf16[16,32,128]{2,1,0:T(8,128)(2,1)S(1)}, u32[]{:S(2)}, u32[]{:S(2)}) collective-permute-start(bf16[16,32,128]{2,1,0:T(8,128)(2,1)S(1)} %get-tuple-element.61), channel_id=1, source_target_pairs={{0,4},{1,3},{2,6},{3,1},{4,0},{5,7},{6,2},{7,5},{8,12},{9,11},{10,... | collective-permute-start | bytes 393224 | tf_op jit(solution)/shard_map/ppermute | solution.py:48
  99.4 11.5 %collective-permute-done.18 = bf16[16,32,128]{2,1,0:T(8,128)(2,1)S(1)} collective-permute-done((bf16[16,32,128]{2,1,0:T(8,128)(2,1)S(1)}, bf16[16,32,128]{2,1,0:T(8,128)(2,1)S(1)}, u32[]{:S(2)}, u32[]{:S(2)}) %collective-permute-start.18) | collective-permute-done | bytes 131104 | tf_op jit(solution)/shard_map/ppermute | solution.py:48
  110.9 3.0 %collective-permute-start.19 = (bf16[32,32,128]{2,1,0:T(8,128)(2,1)S(1)}, bf16[32,32,128]{2,1,0:T(8,128)(2,1)S(1)}, u32[]{:S(2)}, u32[]{:S(2)}) collective-permute-start(bf16[32,32,128]{2,1,0:T(8,128)(2,1)S(1)} %constant_dynamic-update-slice_fusion.refs_0_), channel_id=1, source_target_pairs={{0,2},{1,5},{2,0},{3,7},{4,6},{5,1},{6,4},{7,3},{8,10},{9,13},{10,... | collective-permute-start | bytes 786440 | tf_op jit(solution)/shard_map/ppermute | solution.py:48
  114.4 5.6 %collective-permute-done.19.refs_1_ = bf16[32,32,128]{2,1,0:T(8,128)(2,1)S(1)} collective-permute-done((bf16[32,32,128]{2,1,0:T(8,128)(2,1)S(1)}, bf16[32,32,128]{2,1,0:T(8,128)(2,1)S(1)}, u32[]{:S(2)}, u32[]{:S(2)}) %collective-permute-start.19) | collective-permute-done | bytes 262176 | tf_op jit(solution)/shard_map/ppermute | solution.py:48
  120.7 4.8 %fore.5 = (bf16[2,32,1024]{2,1,0:T(8,128)(2,1)S(1)}, bf16[2,32,1024]{2,1,0:T(8,128)(2,1)S(1)}, bf16[2,32,1024]{2,1,0:T(8,128)(2,1)S(1)}, bf16[2,32,1024]{2,1,0:T(8,128)(2,1)S(1)}) custom-call(s32[1]{0:T(128)} %copy.18.live_ref, s32[192]{0:T(256)S(1)} %get-tuple-element.93.vox_ref, s32[192]{0:T(256)S(1)} %get-tuple-element.76.ray_ref, ...), custom_call_target="tpu_custom_call" | custom-call | flops 8000000000 | tf_op jit(solution)/shard_map/fore/pallas_call | solution.py:332
  125.5 2.3 %collective-permute-start.36 = (bf16[2,32,1024]{2,1,0:T(8,128)(2,1)S(1)}, bf16[2,32,1024]{2,1,0:T(8,128)(2,1)S(1)}, u32[]{:S(2)}, u32[]{:S(2)}) collective-permute-start(bf16[2,32,1024]{2,1,0:T(8,128)(2,1)S(1)} %get-tuple-element.73), channel_id=1, source_target_pairs={{0,8},{8,0},{16,24},{24,16},{1,9},{9,1},{17,25},{25,17},{2,10},{10... | collective-permute-start | bytes 393224 | tf_op jit(solution)/shard_map/ppermute | solution.py:57
  127.8 1.5 collective-permute-start.38
  129.3 6.2 %fore.4 = (bf16[2,64,1024]{2,1,0:T(8,128)(2,1)S(1)}, bf16[2,64,1024]{2,1,0:T(8,128)(2,1)S(1)}, bf16[2,64,1024]{2,1,0:T(8,128)(2,1)S(1)}, bf16[2,64,1024]{2,1,0:T(8,128)(2,1)S(1)}) custom-call(s32[1]{0:T(128)} %copy.18.live_ref, s32[192]{0:T(256)S(1)} %get-tuple-element.93.vox_ref, s32[192]{0:T(256)S(1)} %get-tuple-element.76.ray_ref, ...), custom_call_target="tpu_custom_call" | custom-call | flops 8000000000 | tf_op jit(solution)/shard_map/fore/pallas_call | solution.py:332
  135.5 2.0 %collective-permute-start.29 = (bf16[2,64,1024]{2,1,0:T(8,128)(2,1)S(1)}, bf16[2,64,1024]{2,1,0:T(8,128)(2,1)S(1)}, u32[]{:S(2)}, u32[]{:S(2)}) collective-permute-start(bf16[2,64,1024]{2,1,0:T(8,128)(2,1)S(1)} %get-tuple-element.68), channel_id=1, source_target_pairs={{0,8},{8,0},{16,24},{24,16},{1,9},{9,1},{17,25},{25,17},{2,10},{10... | collective-permute-start | bytes 786440 | tf_op jit(solution)/shard_map/ppermute | solution.py:57
  137.5 4.8 %fore.3 = (bf16[2,32,1024]{2,1,0:T(8,128)(2,1)S(1)}, bf16[2,32,1024]{2,1,0:T(8,128)(2,1)S(1)}, bf16[2,32,1024]{2,1,0:T(8,128)(2,1)S(1)}, bf16[2,32,1024]{2,1,0:T(8,128)(2,1)S(1)}) custom-call(s32[1]{0:T(128)} %copy.18.live_ref, s32[192]{0:T(256)S(1)} %get-tuple-element.93.vox_ref, s32[192]{0:T(256)S(1)} %get-tuple-element.76.ray_ref, ...), custom_call_target="tpu_custom_call" | custom-call | flops 8000000000 | tf_op jit(solution)/shard_map/fore/pallas_call | solution.py:332
  142.5 1.8 %collective-permute-start.23 = (bf16[2,32,1024]{2,1,0:T(8,128)(2,1)S(1)}, bf16[2,32,1024]{2,1,0:T(8,128)(2,1)S(1)}, u32[]{:S(2)}, u32[]{:S(2)}) collective-permute-start(bf16[2,32,1024]{2,1,0:T(8,128)(2,1)S(1)} %get-tuple-element.64), channel_id=1, source_target_pairs={{0,16},{8,24},{16,0},{24,8},{1,17},{9,25},{17,1},{25,9},{2,18},{10... | collective-permute-start | bytes 393224 | tf_op jit(solution)/shard_map/ppermute | solution.py:57
  144.5 1.4 collective-permute-start.31
  146.0 0.8 place.3.refs_4_
  146.8 1.5 collective-permute-start.24
  148.4 1.0 pad_maximum_fusion
  149.4 12.0 %collective-permute-done.30.refs_2_ = bf16[2,64,1024]{2,1,0:T(8,128)(2,1)S(1)} collective-permute-done((bf16[2,64,1024]{2,1,0:T(8,128)(2,1)S(1)}, bf16[2,64,1024]{2,1,0:T(8,128)(2,1)S(1)}, u32[]{:S(2)}, u32[]{:S(2)}) %collective-permute-start.30) | collective-permute-done | bytes 262176 | tf_op jit(solution)/shard_map/ppermute | solution.py:57
  161.4 1.0 place.4.refs_4_
  162.4 0.8 place.5
  (81 shorter events, 3.2 us)
Async XLA Ops:
  0.6 6.8 %copy-start.1 = (bf16[512,512]{1,0:T(8,128)(2,1)S(1)}, bf16[512,512]{1,0:T(8,128)(2,1)}, u32[]{:S(2)}) copy-start(bf16[512,512]{1,0:T(8,128)(2,1)} %slice_ref.3) | copy-start | bytes 1572868
  9.0 7.5 %copy-start.7 = (bf16[2,32,1024]{2,1,0:T(8,128)(2,1)S(1)}, bf16[2,32,1024]{2,1,0:T(8,128)(2,1)}, u32[]{:S(2)}) copy-start(bf16[2,32,1024]{2,1,0:T(8,128)(2,1)} %get-tuple-element.41) | copy-start | bytes 393220
  9.0 9.7 %copy-start.4 = (s32[192]{0:T(256)S(1)}, s32[192]{0:T(256)}, u32[]{:S(2)}) copy-start(s32[192]{0:T(256)} %param.15) | copy-start | bytes 2308
  9.0 9.7 %copy-start.5 = (s32[192]{0:T(256)S(1)}, s32[192]{0:T(256)}, u32[]{:S(2)}) copy-start(s32[192]{0:T(256)} %param.16) | copy-start | bytes 2308
  9.0 11.2 %copy-start.6 = (bf16[2,32,1024]{2,1,0:T(8,128)(2,1)S(1)}, bf16[2,32,1024]{2,1,0:T(8,128)(2,1)}, u32[]{:S(2)}) copy-start(bf16[2,32,1024]{2,1,0:T(8,128)(2,1)} %get-tuple-element.42) | copy-start | bytes 393220
  10.0 10.2 %collective-permute-start.6 = (bf16[2,64,1024]{2,1,0:T(8,128)(2,1)S(1)}, bf16[2,64,1024]{2,1,0:T(8,128)(2,1)S(1)}, u32[]{:S(2)}, u32[]{:S(2)}) collective-permute-start(bf16[2,64,1024]{2,1,0:T(8,128)(2,1)S(1)} %get-tuple-element.48), channel_id=1, source_target_pairs={{0,8},{8,0},{16,24},{24,16},{1,9},{9,1},{17,25},{25,17},{2,10},{10... | collective-permute-start | bytes 786440 | tf_op jit(solution)/shard_map/ppermute | solution.py:57
  13.1 14.8 %collective-permute-start.7 = (bf16[2,64,1024]{2,1,0:T(8,128)(2,1)S(1)}, bf16[2,64,1024]{2,1,0:T(8,128)(2,1)S(1)}, u32[]{:S(2)}, u32[]{:S(2)}) collective-permute-start(bf16[2,64,1024]{2,1,0:T(8,128)(2,1)S(1)} %get-tuple-element.49), channel_id=1, source_target_pairs={{0,16},{8,24},{16,0},{24,8},{1,17},{9,25},{17,1},{25,9},{2,18},{10... | collective-permute-start | bytes 786440 | tf_op jit(solution)/shard_map/ppermute | solution.py:57
  14.6 13.3 %collective-permute-start.8 = (bf16[2,64,1024]{2,1,0:T(8,128)(2,1)S(1)}, bf16[2,64,1024]{2,1,0:T(8,128)(2,1)S(1)}, u32[]{:S(2)}, u32[]{:S(2)}) collective-permute-start(bf16[2,64,1024]{2,1,0:T(8,128)(2,1)S(1)} %get-tuple-element.50), channel_id=1, source_target_pairs={{0,24},{8,16},{16,8},{24,0},{1,25},{9,17},{17,9},{25,1},{2,26},{10... | collective-permute-start | bytes 786440 | tf_op jit(solution)/shard_map/ppermute | solution.py:57
  14.6 20.4 %collective-permute-start = (bf16[2,32,1024]{2,1,0:T(8,128)(2,1)S(1)}, bf16[2,32,1024]{2,1,0:T(8,128)(2,1)S(1)}, u32[]{:S(2)}, u32[]{:S(2)}) collective-permute-start(bf16[2,32,1024]{2,1,0:T(8,128)(2,1)S(1)} %copy-done.8), channel_id=1, source_target_pairs={{0,8},{8,0},{16,24},{24,16},{1,9},{9,1},{17,25},{25,17},{2,10},{10... | collective-permute-start | bytes 393224 | tf_op jit(solution)/shard_map/ppermute | solution.py:57
  16.5 20.0 %collective-permute-start.1 = (bf16[2,32,1024]{2,1,0:T(8,128)(2,1)S(1)}, bf16[2,32,1024]{2,1,0:T(8,128)(2,1)S(1)}, u32[]{:S(2)}, u32[]{:S(2)}) collective-permute-start(bf16[2,32,1024]{2,1,0:T(8,128)(2,1)S(1)} %copy-done.7), channel_id=1, source_target_pairs={{0,16},{8,24},{16,0},{24,8},{1,17},{9,25},{17,1},{25,9},{2,18},{10... | collective-permute-start | bytes 393224 | tf_op jit(solution)/shard_map/ppermute | solution.py:57
  20.2 16.3 %collective-permute-start.2 = (bf16[2,32,1024]{2,1,0:T(8,128)(2,1)S(1)}, bf16[2,32,1024]{2,1,0:T(8,128)(2,1)S(1)}, u32[]{:S(2)}, u32[]{:S(2)}) collective-permute-start(bf16[2,32,1024]{2,1,0:T(8,128)(2,1)S(1)} %copy-done.6), channel_id=1, source_target_pairs={{0,24},{8,16},{16,8},{24,0},{1,25},{9,17},{17,9},{25,1},{2,26},{10... | collective-permute-start | bytes 393224 | tf_op jit(solution)/shard_map/ppermute | solution.py:57
  27.8 13.8 %collective-permute-start.12 = (bf16[2,32,1024]{2,1,0:T(8,128)(2,1)S(1)}, bf16[2,32,1024]{2,1,0:T(8,128)(2,1)S(1)}, u32[]{:S(2)}, u32[]{:S(2)}) collective-permute-start(bf16[2,32,1024]{2,1,0:T(8,128)(2,1)S(1)} %get-tuple-element.55), channel_id=1, source_target_pairs={{0,8},{8,0},{16,24},{24,16},{1,9},{9,1},{17,25},{25,17},{2,10},{10... | collective-permute-start | bytes 393224 | tf_op jit(solution)/shard_map/ppermute | solution.py:57
  27.9 13.8 %collective-permute-start.13 = (bf16[2,32,1024]{2,1,0:T(8,128)(2,1)S(1)}, bf16[2,32,1024]{2,1,0:T(8,128)(2,1)S(1)}, u32[]{:S(2)}, u32[]{:S(2)}) collective-permute-start(bf16[2,32,1024]{2,1,0:T(8,128)(2,1)S(1)} %get-tuple-element.56), channel_id=1, source_target_pairs={{0,16},{8,24},{16,0},{24,8},{1,17},{9,25},{17,1},{25,9},{2,18},{10... | collective-permute-start | bytes 393224 | tf_op jit(solution)/shard_map/ppermute | solution.py:57
  30.2 6.3 %copy-start.3 = (bf16[2,32,1024]{2,1,0:T(8,128)(2,1)S(1)}, bf16[2,32,1024]{2,1,0:T(8,128)(2,1)}, u32[]{:S(2)}) copy-start(bf16[2,32,1024]{2,1,0:T(8,128)(2,1)} %get-tuple-element.39.refs_0_) | copy-start | bytes 393220
  35.0 6.6 %collective-permute-start.14 = (bf16[2,32,1024]{2,1,0:T(8,128)(2,1)S(1)}, bf16[2,32,1024]{2,1,0:T(8,128)(2,1)S(1)}, u32[]{:S(2)}, u32[]{:S(2)}) collective-permute-start(bf16[2,32,1024]{2,1,0:T(8,128)(2,1)S(1)} %get-tuple-element.57), channel_id=1, source_target_pairs={{0,24},{8,16},{16,8},{24,0},{1,25},{9,17},{17,9},{25,1},{2,26},{10... | collective-permute-start | bytes 393224 | tf_op jit(solution)/shard_map/ppermute | solution.py:57
  36.5 9.8 %collective-permute-start.9 = (bf16[64,64,128]{2,1,0:T(8,128)(2,1)S(1)}, bf16[64,64,128]{2,1,0:T(8,128)(2,1)S(1)}, u32[]{:S(2)}, u32[]{:S(2)}) collective-permute-start(bf16[64,64,128]{2,1,0:T(8,128)(2,1)S(1)} %get-tuple-element.52), channel_id=1, source_target_pairs={{0,1},{1,0},{2,3},{3,2},{4,5},{5,4},{6,7},{7,6},{8,9},{9,8},{10,11... | collective-permute-start | bytes 3145736 | tf_op jit(solution)/shard_map/ppermute | solution.py:57
  41.0 7.0 %collective-permute-start.3 = (bf16[64,32,128]{2,1,0:T(8,128)(2,1)S(1)}, bf16[64,32,128]{2,1,0:T(8,128)(2,1)S(1)}, u32[]{:S(2)}, u32[]{:S(2)}) collective-permute-start(bf16[64,32,128]{2,1,0:T(8,128)(2,1)S(1)} %get-tuple-element.44), channel_id=1, source_target_pairs={{0,1},{1,0},{2,3},{3,2},{4,5},{5,4},{6,7},{7,6},{8,9},{9,8},{10,11... | collective-permute-start | bytes 1572872 | tf_op jit(solution)/shard_map/ppermute | solution.py:57
  46.3 2.8 %collective-permute-start.15 = (bf16[64,32,128]{2,1,0:T(8,128)(2,1)S(1)}, bf16[64,32,128]{2,1,0:T(8,128)(2,1)S(1)}, u32[]{:S(2)}, u32[]{:S(2)}) collective-permute-start(bf16[64,32,128]{2,1,0:T(8,128)(2,1)S(1)} %get-tuple-element.59), channel_id=1, source_target_pairs={{0,1},{1,0},{2,3},{3,2},{4,5},{5,4},{6,7},{7,6},{8,9},{9,8},{10,11... | collective-permute-start | bytes 1572872 | tf_op jit(solution)/shard_map/ppermute | solution.py:57
  46.8 22.7 %collective-permute-start.10 = (bf16[32,64,128]{2,1,0:T(8,128)(2,1)S(1)}, bf16[32,64,128]{2,1,0:T(8,128)(2,1)S(1)}, u32[]{:S(2)}, u32[]{:S(2)}) collective-permute-start(bf16[32,64,128]{2,1,0:T(8,128)(2,1)S(1)} %get-tuple-element.81), channel_id=1, source_target_pairs={{0,2},{1,5},{2,0},{3,7},{4,6},{5,1},{6,4},{7,3},{8,10},{9,13},{10,... | collective-permute-start | bytes 1572872 | tf_op jit(solution)/shard_map/ppermute | solution.py:48
  48.2 18.9 %collective-permute-start.4 = (bf16[32,32,128]{2,1,0:T(8,128)(2,1)S(1)}, bf16[32,32,128]{2,1,0:T(8,128)(2,1)S(1)}, u32[]{:S(2)}, u32[]{:S(2)}) collective-permute-start(bf16[32,32,128]{2,1,0:T(8,128)(2,1)S(1)} %get-tuple-element.83), channel_id=1, source_target_pairs={{0,2},{1,5},{2,0},{3,7},{4,6},{5,1},{6,4},{7,3},{8,10},{9,13},{10,... | collective-permute-start | bytes 786440 | tf_op jit(solution)/shard_map/ppermute | solution.py:48
  49.1 27.3 %copy-start = (f32[128,2048]{1,0:T(8,128)S(1)}, f32[128,2048]{1,0:T(8,128)}, u32[]{:S(2)}) copy-start(f32[128,2048]{1,0:T(8,128)} %volume_ref.5) | copy-start | bytes 3145732
  49.2 27.0 %collective-permute-start.16 = (bf16[32,32,128]{2,1,0:T(8,128)(2,1)S(1)}, bf16[32,32,128]{2,1,0:T(8,128)(2,1)S(1)}, u32[]{:S(2)}, u32[]{:S(2)}) collective-permute-start(bf16[32,32,128]{2,1,0:T(8,128)(2,1)S(1)} %get-tuple-element.87), channel_id=1, source_target_pairs={{0,2},{1,5},{2,0},{3,7},{4,6},{5,1},{6,4},{7,3},{8,10},{9,13},{10,... | collective-permute-start | bytes 786440 | tf_op jit(solution)/shard_map/ppermute | solution.py:48
  67.1 9.3 %collective-permute-start.5 = (bf16[16,32,128]{2,1,0:T(8,128)(2,1)S(1)}, bf16[16,32,128]{2,1,0:T(8,128)(2,1)S(1)}, u32[]{:S(2)}, u32[]{:S(2)}) collective-permute-start(bf16[16,32,128]{2,1,0:T(8,128)(2,1)S(1)} %get-tuple-element.88), channel_id=1, source_target_pairs={{0,4},{1,3},{2,6},{3,1},{4,0},{5,7},{6,2},{7,5},{8,12},{9,11},{10,... | collective-permute-start | bytes 393224 | tf_op jit(solution)/shard_map/ppermute | solution.py:48
  69.6 11.0 %collective-permute-start.11 = (bf16[16,64,128]{2,1,0:T(8,128)(2,1)S(1)}, bf16[16,64,128]{2,1,0:T(8,128)(2,1)S(1)}, u32[]{:S(2)}, u32[]{:S(2)}) collective-permute-start(bf16[16,64,128]{2,1,0:T(8,128)(2,1)S(1)} %get-tuple-element.84), channel_id=1, source_target_pairs={{0,4},{1,3},{2,6},{3,1},{4,0},{5,7},{6,2},{7,5},{8,12},{9,11},{10,... | collective-permute-start | bytes 786440 | tf_op jit(solution)/shard_map/ppermute | solution.py:48
  76.3 19.0 %collective-permute-start.17 = (bf16[16,32,128]{2,1,0:T(8,128)(2,1)S(1)}, bf16[16,32,128]{2,1,0:T(8,128)(2,1)S(1)}, u32[]{:S(2)}, u32[]{:S(2)}) collective-permute-start(bf16[16,32,128]{2,1,0:T(8,128)(2,1)S(1)} %get-tuple-element.90), channel_id=1, source_target_pairs={{0,4},{1,3},{2,6},{3,1},{4,0},{5,7},{6,2},{7,5},{8,12},{9,11},{10,... | collective-permute-start | bytes 393224 | tf_op jit(solution)/shard_map/ppermute | solution.py:48
  76.4 44.2 %slice-start = ((s8[6291456]{0:T(1024)(128)(4,1)}), s8[4194304]{0:T(1024)(128)(4,1)S(1)}, s32[]{:S(2)}) async-start(s8[6291456]{0:T(1024)(128)(4,1)} %bitcast.2), calls=%async_computation | async-start | bytes 8388608
  76.5 10.0 %collective-permute-start.32 = (bf16[16,32,128]{2,1,0:T(8,128)(2,1)S(1)}, bf16[16,32,128]{2,1,0:T(8,128)(2,1)S(1)}, u32[]{:S(2)}, u32[]{:S(2)}) collective-permute-start(bf16[16,32,128]{2,1,0:T(8,128)(2,1)S(1)} %get-tuple-element.71), channel_id=1, source_target_pairs={{0,4},{1,3},{2,6},{3,1},{4,0},{5,7},{6,2},{7,5},{8,12},{9,11},{10,... | collective-permute-start | bytes 393224 | tf_op jit(solution)/shard_map/ppermute | solution.py:48
  80.6 40.1 %slice-start.1 = ((s8[6291456]{0:T(1024)(128)(4,1)}), s8[2097152]{0:T(1024)(128)(4,1)S(1)}, s32[]{:S(2)}) async-start(s8[6291456]{0:T(1024)(128)(4,1)} %bitcast.2), calls=%async_computation.1 | async-start | bytes 4194304
  80.7 12.3 %collective-permute-start.25 = (bf16[16,64,128]{2,1,0:T(8,128)(2,1)S(1)}, bf16[16,64,128]{2,1,0:T(8,128)(2,1)S(1)}, u32[]{:S(2)}, u32[]{:S(2)}) collective-permute-start(bf16[16,64,128]{2,1,0:T(8,128)(2,1)S(1)} %get-tuple-element.66), channel_id=1, source_target_pairs={{0,4},{1,3},{2,6},{3,1},{4,0},{5,7},{6,2},{7,5},{8,12},{9,11},{10,... | collective-permute-start | bytes 786440 | tf_op jit(solution)/shard_map/ppermute | solution.py:48
  86.5 27.4 %collective-permute-start.33 = (bf16[32,32,128]{2,1,0:T(8,128)(2,1)S(1)}, bf16[32,32,128]{2,1,0:T(8,128)(2,1)S(1)}, u32[]{:S(2)}, u32[]{:S(2)}) collective-permute-start(bf16[32,32,128]{2,1,0:T(8,128)(2,1)S(1)} %constant_dynamic-update-slice_fusion.4.refs_0_), channel_id=1, source_target_pairs={{0,2},{1,5},{2,0},{3,7},{4,6},{5,1},{6,4},{7,3},{8,10},{9,13},{10,... | collective-permute-start | bytes 786440 | tf_op jit(solution)/shard_map/ppermute | solution.py:48
  93.1 27.5 %collective-permute-start.26 = (bf16[32,64,128]{2,1,0:T(8,128)(2,1)S(1)}, bf16[32,64,128]{2,1,0:T(8,128)(2,1)S(1)}, u32[]{:S(2)}, u32[]{:S(2)}) collective-permute-start(bf16[32,64,128]{2,1,0:T(8,128)(2,1)S(1)} %constant_dynamic-update-slice_fusion.2.refs_0_), channel_id=1, source_target_pairs={{0,2},{1,5},{2,0},{3,7},{4,6},{5,1},{6,4},{7,3},{8,10},{9,13},{10,... | collective-permute-start | bytes 1572872 | tf_op jit(solution)/shard_map/ppermute | solution.py:48
  95.4 15.4 %collective-permute-start.18 = (bf16[16,32,128]{2,1,0:T(8,128)(2,1)S(1)}, bf16[16,32,128]{2,1,0:T(8,128)(2,1)S(1)}, u32[]{:S(2)}, u32[]{:S(2)}) collective-permute-start(bf16[16,32,128]{2,1,0:T(8,128)(2,1)S(1)} %get-tuple-element.61), channel_id=1, source_target_pairs={{0,4},{1,3},{2,6},{3,1},{4,0},{5,7},{6,2},{7,5},{8,12},{9,11},{10,... | collective-permute-start | bytes 393224 | tf_op jit(solution)/shard_map/ppermute | solution.py:48
  110.9 9.2 %collective-permute-start.19 = (bf16[32,32,128]{2,1,0:T(8,128)(2,1)S(1)}, bf16[32,32,128]{2,1,0:T(8,128)(2,1)S(1)}, u32[]{:S(2)}, u32[]{:S(2)}) collective-permute-start(bf16[32,32,128]{2,1,0:T(8,128)(2,1)S(1)} %constant_dynamic-update-slice_fusion.refs_0_), channel_id=1, source_target_pairs={{0,2},{1,5},{2,0},{3,7},{4,6},{5,1},{6,4},{7,3},{8,10},{9,13},{10,... | collective-permute-start | bytes 786440 | tf_op jit(solution)/shard_map/ppermute | solution.py:48
  113.9 6.2 %collective-permute-start.34 = (bf16[32,32,128]{2,1,0:T(8,128)(2,1)S(1)}, bf16[32,32,128]{2,1,0:T(8,128)(2,1)S(1)}, u32[]{:S(2)}, u32[]{:S(2)}) collective-permute-start(bf16[32,32,128]{2,1,0:T(8,128)(2,1)S(1)} %constant_dynamic-update-slice_fusion.4.refs_0_), channel_id=1, source_target_pairs={{0,1},{1,0},{2,3},{3,2},{4,5},{5,4},{6,7},{7,6},{8,9},{9,8},{10,11... | collective-permute-start | bytes 786440 | tf_op jit(solution)/shard_map/ppermute | solution.py:57
  113.9 6.8 %collective-permute-start.35 = (bf16[32,32,128]{2,1,0:T(8,128)(2,1)S(1)}, bf16[32,32,128]{2,1,0:T(8,128)(2,1)S(1)}, u32[]{:S(2)}, u32[]{:S(2)}) collective-permute-start(bf16[32,32,128]{2,1,0:T(8,128)(2,1)S(1)} %collective-permute-done.33.refs_1_), channel_id=1, source_target_pairs={{0,1},{1,0},{2,3},{3,2},{4,5},{5,4},{6,7},{7,6},{8,9},{9,8},{10,11... | collective-permute-start | bytes 786440 | tf_op jit(solution)/shard_map/ppermute | solution.py:57
  114.4 21.1 %collective-permute-start.20 = (bf16[32,32,128]{2,1,0:T(8,128)(2,1)S(1)}, bf16[32,32,128]{2,1,0:T(8,128)(2,1)S(1)}, u32[]{:S(2)}, u32[]{:S(2)}) collective-permute-start(bf16[32,32,128]{2,1,0:T(8,128)(2,1)S(1)} %constant_dynamic-update-slice_fusion.refs_0_), channel_id=1, source_target_pairs={{0,1},{1,0},{2,3},{3,2},{4,5},{5,4},{6,7},{7,6},{8,9},{9,8},{10,11... | collective-permute-start | bytes 786440 | tf_op jit(solution)/shard_map/ppermute | solution.py:57
  120.1 17.5 %collective-permute-start.21 = (bf16[32,32,128]{2,1,0:T(8,128)(2,1)S(1)}, bf16[32,32,128]{2,1,0:T(8,128)(2,1)S(1)}, u32[]{:S(2)}, u32[]{:S(2)}) collective-permute-start(bf16[32,32,128]{2,1,0:T(8,128)(2,1)S(1)} %collective-permute-done.19.refs_1_), channel_id=1, source_target_pairs={{0,1},{1,0},{2,3},{3,2},{4,5},{5,4},{6,7},{7,6},{8,9},{9,8},{10,11... | collective-permute-start | bytes 786440 | tf_op jit(solution)/shard_map/ppermute | solution.py:57
  120.1 7.7 %collective-permute-start.27 = (bf16[32,64,128]{2,1,0:T(8,128)(2,1)S(1)}, bf16[32,64,128]{2,1,0:T(8,128)(2,1)S(1)}, u32[]{:S(2)}, u32[]{:S(2)}) collective-permute-start(bf16[32,64,128]{2,1,0:T(8,128)(2,1)S(1)} %constant_dynamic-update-slice_fusion.2.refs_0_), channel_id=1, source_target_pairs={{0,1},{1,0},{2,3},{3,2},{4,5},{5,4},{6,7},{7,6},{8,9},{9,8},{10,11... | collective-permute-start | bytes 1572872 | tf_op jit(solution)/shard_map/ppermute | solution.py:57
  120.6 7.2 %collective-permute-start.28 = (bf16[32,64,128]{2,1,0:T(8,128)(2,1)S(1)}, bf16[32,64,128]{2,1,0:T(8,128)(2,1)S(1)}, u32[]{:S(2)}, u32[]{:S(2)}) collective-permute-start(bf16[32,64,128]{2,1,0:T(8,128)(2,1)S(1)} %collective-permute-done.26.refs_1_), channel_id=1, source_target_pairs={{0,1},{1,0},{2,3},{3,2},{4,5},{5,4},{6,7},{7,6},{8,9},{9,8},{10,11... | collective-permute-start | bytes 1572872 | tf_op jit(solution)/shard_map/ppermute | solution.py:57
  125.5 17.0 %collective-permute-start.36 = (bf16[2,32,1024]{2,1,0:T(8,128)(2,1)S(1)}, bf16[2,32,1024]{2,1,0:T(8,128)(2,1)S(1)}, u32[]{:S(2)}, u32[]{:S(2)}) collective-permute-start(bf16[2,32,1024]{2,1,0:T(8,128)(2,1)S(1)} %get-tuple-element.73), channel_id=1, source_target_pairs={{0,8},{8,0},{16,24},{24,16},{1,9},{9,1},{17,25},{25,17},{2,10},{10... | collective-permute-start | bytes 393224 | tf_op jit(solution)/shard_map/ppermute | solution.py:57
  127.8 16.5 %collective-permute-start.37 = (bf16[2,32,1024]{2,1,0:T(8,128)(2,1)S(1)}, bf16[2,32,1024]{2,1,0:T(8,128)(2,1)S(1)}, u32[]{:S(2)}, u32[]{:S(2)}) collective-permute-start(bf16[2,32,1024]{2,1,0:T(8,128)(2,1)S(1)} %get-tuple-element.74), channel_id=1, source_target_pairs={{0,16},{8,24},{16,0},{24,8},{1,17},{9,25},{17,1},{25,9},{2,18},{10... | collective-permute-start | bytes 393224 | tf_op jit(solution)/shard_map/ppermute | solution.py:57
  127.8 16.8 %collective-permute-start.38 = (bf16[2,32,1024]{2,1,0:T(8,128)(2,1)S(1)}, bf16[2,32,1024]{2,1,0:T(8,128)(2,1)S(1)}, u32[]{:S(2)}, u32[]{:S(2)}) collective-permute-start(bf16[2,32,1024]{2,1,0:T(8,128)(2,1)S(1)} %get-tuple-element.75), channel_id=1, source_target_pairs={{0,24},{8,16},{16,8},{24,0},{1,25},{9,17},{17,9},{25,1},{2,26},{10... | collective-permute-start | bytes 393224 | tf_op jit(solution)/shard_map/ppermute | solution.py:57
  135.5 11.3 %collective-permute-start.29 = (bf16[2,64,1024]{2,1,0:T(8,128)(2,1)S(1)}, bf16[2,64,1024]{2,1,0:T(8,128)(2,1)S(1)}, u32[]{:S(2)}, u32[]{:S(2)}) collective-permute-start(bf16[2,64,1024]{2,1,0:T(8,128)(2,1)S(1)} %get-tuple-element.68), channel_id=1, source_target_pairs={{0,8},{8,0},{16,24},{24,16},{1,9},{9,1},{17,25},{25,17},{2,10},{10... | collective-permute-start | bytes 786440 | tf_op jit(solution)/shard_map/ppermute | solution.py:57
  142.3 20.0 %collective-permute-start.22 = (bf16[2,32,1024]{2,1,0:T(8,128)(2,1)S(1)}, bf16[2,32,1024]{2,1,0:T(8,128)(2,1)S(1)}, u32[]{:S(2)}, u32[]{:S(2)}) collective-permute-start(bf16[2,32,1024]{2,1,0:T(8,128)(2,1)S(1)} %get-tuple-element.63), channel_id=1, source_target_pairs={{0,8},{8,0},{16,24},{24,16},{1,9},{9,1},{17,25},{25,17},{2,10},{10... | collective-permute-start | bytes 393224 | tf_op jit(solution)/shard_map/ppermute | solution.py:57
  142.5 19.9 %collective-permute-start.23 = (bf16[2,32,1024]{2,1,0:T(8,128)(2,1)S(1)}, bf16[2,32,1024]{2,1,0:T(8,128)(2,1)S(1)}, u32[]{:S(2)}, u32[]{:S(2)}) collective-permute-start(bf16[2,32,1024]{2,1,0:T(8,128)(2,1)S(1)} %get-tuple-element.64), channel_id=1, source_target_pairs={{0,16},{8,24},{16,0},{24,8},{1,17},{9,25},{17,1},{25,9},{2,18},{10... | collective-permute-start | bytes 393224 | tf_op jit(solution)/shard_map/ppermute | solution.py:57
  144.3 17.1 %collective-permute-start.30 = (bf16[2,64,1024]{2,1,0:T(8,128)(2,1)S(1)}, bf16[2,64,1024]{2,1,0:T(8,128)(2,1)S(1)}, u32[]{:S(2)}, u32[]{:S(2)}) collective-permute-start(bf16[2,64,1024]{2,1,0:T(8,128)(2,1)S(1)} %get-tuple-element.69), channel_id=1, source_target_pairs={{0,16},{8,24},{16,0},{24,8},{1,17},{9,25},{17,1},{25,9},{2,18},{10... | collective-permute-start | bytes 786440 | tf_op jit(solution)/shard_map/ppermute | solution.py:57
  144.5 16.8 %collective-permute-start.31 = (bf16[2,64,1024]{2,1,0:T(8,128)(2,1)S(1)}, bf16[2,64,1024]{2,1,0:T(8,128)(2,1)S(1)}, u32[]{:S(2)}, u32[]{:S(2)}) collective-permute-start(bf16[2,64,1024]{2,1,0:T(8,128)(2,1)S(1)} %get-tuple-element.70), channel_id=1, source_target_pairs={{0,24},{8,16},{16,8},{24,0},{1,25},{9,17},{17,9},{25,1},{2,26},{10... | collective-permute-start | bytes 786440 | tf_op jit(solution)/shard_map/ppermute | solution.py:57
  146.8 15.6 %collective-permute-start.24 = (bf16[2,32,1024]{2,1,0:T(8,128)(2,1)S(1)}, bf16[2,32,1024]{2,1,0:T(8,128)(2,1)S(1)}, u32[]{:S(2)}, u32[]{:S(2)}) collective-permute-start(bf16[2,32,1024]{2,1,0:T(8,128)(2,1)S(1)} %get-tuple-element.65), channel_id=1, source_target_pairs={{0,24},{8,16},{16,8},{24,0},{1,25},{9,17},{17,9},{25,1},{2,26},{10... | collective-permute-start | bytes 393224 | tf_op jit(solution)/shard_map/ppermute | solution.py:57
  (2 other events, 7.2 us)
